TPU v7x, 32 devices: a whole 2x2x4 slice. The times are simulated.
32 devices in a mesh: occ: 8 (over z, x), aux: 4 (over y, core).
Axes of the slice: x: 2, y: 2, z: 4, core: 2. Of those that a mesh axis runs over, the one named last changes fastest.
Arguments:
- half_integrals: bfloat16 [8, 1024, 1024], P(None, 'aux'), may hold values from -1 to 1
- vir_coef: bfloat16 [1024, 768], P(None, 'occ'), may hold values from -0.1875 to 0.1875
- occ_energy: float32 [8], replicated, may hold values from -3 to -0.3
- vir_energy: float32 [768], replicated, may hold values from 0.1 to 2
Outputs:
- three_index: float32 [1024, 8, 768], P('aux', 'occ')
- vir_density: float32 [768, 768], P(('occ', 'aux'))
All inputs are finite; a program needn't handle non-finite values.
Results may differ from a plain program's by a relative error of at most 0.0006.
The roundings to bfloat16 on the way count: a program that leaves them out, or rounds other values in their place, can miss the bound.
Values may be sent and summed in bfloat16 or wider, within the bound.
A program may use at most 64 MiB of HBM per device.

v0:
```python
import functools

import jax
import jax.numpy as jnp
from jax import lax
from jax.experimental import pallas as pl
from jax.experimental.pallas import tpu as pltpu
from jax.sharding import PartitionSpec as P

MESH = pl.DeviceIdType.MESH
F32 = jnp.float32
LIMIT = 56 * 1024 * 1024


def remote(src, dst, send, recv, target):
    return pltpu.make_async_remote_copy(
        src_ref=src, dst_ref=dst, send_sem=send, recv_sem=recv, device_id=target, device_id_type=MESH
    )


def nearest_first(z, k, count):
    near = jnp.minimum(z, count - 1 - z)
    step = (k + 1) // 2
    both = z + step * (2 * (k % 2) - 1)
    low = z < count - 1 - z
    return jnp.where(k <= 2 * near, both, jnp.where(low, k, count - 1 - k))


def greet(n, nq):
    o = lax.axis_index("occ")
    s = lax.axis_index("aux")
    q, c = s // 2, s % 2
    z, low = o // 2, o % 2
    nz = n // 2
    barrier = pltpu.get_barrier_semaphore()
    peers = [(2 * z + 1 - low, s), (o, 2 * q + 1 - c)]
    peers += [(o, 2 * ((q + d) % nq) + c) for d in range(1, nq)]
    peers += [(2 * ((z + d) % nz) + low, s) for d in range(1, nz)]
    for peer in peers:
        pl.semaphore_signal(barrier, inc=1, device_id=peer, device_id_type=MESH)
    return lambda: pl.semaphore_wait(barrier, len(peers))


def make_densities(
    n, nq, occ_e, half, coef, vir_e, three, vir,
    ints, full, own, held, gift, amps,
    i_sem, c_copy, o_copy, c_recv, c_up, c_down, c_side, cp_send, cp_recv,
    own_send, own_recv, fw_send, fw_recv, pr_send, pr_recv, g_send, g_recv,
    h_recv, h_up, h_down, h_side,
    vir_done=lambda: None,
):
    o = lax.axis_index("occ")
    s = lax.axis_index("aux")
    q, c = s // 2, s % 2
    z, low = o // 2, o % 2
    nz = n // 2
    width = amps.shape[0] // n
    part = coef.shape[0]
    cut = coef.shape[1] // 2
    virtuals = amps.shape[1]
    above, below, side = o + 2, o - 2, 2 * z + 1 - low
    partner = (o, 2 * q + 1 - c)
    entered = greet(n, nq)

    fetch = pltpu.make_async_copy(half, ints, i_sem)
    fetch.start()

    def span(index, size):
        return pl.ds(pl.multiple_of(index * size, size), size)

    def keep(h):
        return pltpu.make_async_copy(coef.at[:, h * cut : (h + 1) * cut], full.at[h, span(o, part)], c_copy.at[h])

    keep(0).start()
    keep(1).start()
    entered()

    def relay(chain, src, dst, up, down, across, recv, act):
        pl.when(jnp.logical_and(chain <= z, z < nz - 1))(lambda: act(remote(src, dst, up, recv, (above, s))))
        pl.when(jnp.logical_and(chain >= z, z > 0))(lambda: act(remote(src, dst, down, recv, (below, s))))
        act(remote(src, dst, across, recv, (side, s)))

    def start(copy):
        copy.start()

    def sent(copy):
        copy.wait_send()

    def coef_slot(block):
        return full.at[c, span(block, part)]

    def coef_relay(chain, src, act):
        block = 2 * chain + low
        relay(chain, src, coef_slot(block), c_up.at[chain], c_down.at[chain], c_side.at[chain], c_recv.at[block], act)

    def coef_across(block):
        return remote(coef_slot(block), coef_slot(block), cp_send.at[block], cp_recv.at[block], partner)

    def coef_arrived(block):
        remote(coef_slot(block), coef_slot(block), c_side.at[0], c_recv.at[block], (side, s)).wait_recv()
        coef_across(block).start()

    coef_relay(z, coef.at[:, span(c, cut)], start)
    three[...] = jnp.zeros_like(three)
    vir[...] = jnp.zeros_like(vir)
    row_e = vir_e[...].reshape(1, virtuals)
    here = lax.broadcasted_iota(jnp.int32, (width, virtuals), 0) + s * width
    there = lax.broadcasted_iota(jnp.int32, (width, virtuals), 1)
    col_e = jnp.sum(jnp.where(here == there, row_e, 0.0), axis=1, keepdims=True)

    @pl.loop(1, nz)
    def _(k):
        chain = nearest_first(z, k, nz)
        block = 2 * chain + low
        remote(coef_slot(block), coef_slot(block), c_side.at[0], c_recv.at[block], (side, s)).wait_recv()
        coef_relay(chain, coef_slot(block), start)
        coef_across(block).start()
        coef_arrived(2 * nearest_first(z, k - 1, nz) + 1 - low)

    coef_arrived(2 * nearest_first(z, nz - 1, nz) + 1 - low)

    @pl.loop(1, n)
    def _(d):
        block = (o + d) % n
        other = full.at[1 - c, span(block, part)]
        remote(other, other, cp_send.at[block], cp_recv.at[block], partner).wait_recv()

    keep(0).wait()
    keep(1).wait()
    fetch.wait()

    def transform(block, rows):
        contract = (((1,), (1,)), ((), ()))
        return sum(
            lax.dot_general(
                full[h, rows, :], ints[block, :, h * cut : (h + 1) * cut], contract, preferred_element_type=F32
            )
            for h in range(2)
        ).astype(jnp.bfloat16)

    order = list(range(1, nq)) + [0]

    def chunk(there, core, group):
        return own.at[there, core, group]

    def to_partner(r):
        ref = chunk(q, c, (q + r) % nq)
        return remote(ref, ref, pr_send.at[r], pr_recv.at[r], partner)

    def to_chip(d, r):
        ref = chunk(q, c, (q + r) % nq)
        return remote(ref, ref, own_send.at[d, r], own_recv.at[d, r], (o, 2 * ((q + d) % nq) + c))

    def onward(d, r, core):
        there = (q + nq - d) % nq
        ref = chunk(there, core, (there + r) % nq)
        return remote(ref, ref, fw_send.at[d, r], fw_recv.at[d, r], partner)

    def from_chip(d, r):
        there = (q + nq - d) % nq
        ref = chunk(there, c, (there + r) % nq)
        remote(ref, ref, own_send.at[d, r], own_recv.at[d, r], partner).wait_recv()
        onward(d, r, c).start()

    for r in order:
        group = (q + r) % nq
        own[q, c, group] = transform(o, span(group, 2 * width))
        for d in range(1, nq):
            to_chip(d, r).start()
        to_partner(r).start()

    def give(block, core):
        return remote(
            gift.at[block], held.at[q, core, span(block, width)], g_send.at[block], g_recv.at[block], partner
        )

    @pl.loop(1, n)
    def _(d):
        block = (o + d) % n
        gift[block] = transform(block, span(2 * q + 1 - c, width))
        give(block, c).start()
        held[q, c, span(block, width), :] = transform(block, span(s, width))

    def held_slot(d, block):
        return held.at[(q + nq - d) % nq, :, span(block, width)]

    def own_slot(d):
        return own.at[(q + nq - d) % nq, :, q, span(c, width)]

    def held_relay(d, chain, src, act):
        block = 2 * chain + low
        relay(
            chain, src, held_slot(d, block), h_up.at[d, chain], h_down.at[d, chain], h_side.at[d, chain],
            h_recv.at[d, block], act,
        )

    def arrived(block):
        for d in range(1, nq):
            ref = held_slot(d, block)
            remote(ref, ref, h_side.at[d, 0], h_recv.at[d, block], (side, s)).wait_recv()

    for d in range(1, nq):
        from_chip(d, d)
    for d in range(1, nq):
        onward(d, d, 1 - c).wait_recv()
        held_relay(d, z, own_slot(d), start)
    rest = [(d, r) for d in range(1, nq) for r in order if r != d]
    for d, r in rest:
        from_chip(d, r)
    for r in order:
        ref = chunk(q, 1 - c, (q + r) % nq)
        remote(ref, ref, pr_send.at[r], pr_recv.at[r], partner).wait_recv()

    @pl.loop(1, n)
    def _(d):
        give((o + d) % n, 1 - c).wait_recv()

    for d, r in rest:
        onward(d, r, 1 - c).wait_recv()
    mine = pltpu.make_async_copy(
        own.at[:, :, q, span(c, width)], held.at[:, :, span(o, width)], o_copy
    )
    mine.start()
    mine.wait()

    def absorb(block):
        rows = span(block, width)
        coulomb = sum(
            lax.dot_general(
                held[t // 2, t % 2, rows, :], own[t // 2, t % 2].reshape(virtuals, -1),
                (((1,), (1,)), ((), ())), preferred_element_type=F32,
            )
            for t in range(2 * nq)
        )
        denominator = occ_e[o] + occ_e[block] - col_e - row_e
        amps[rows, :] = (coulomb / denominator).astype(jnp.bfloat16)

    contract = (((0,), (0,)), ((), ()))
    piece = virtuals // 2 if len(vir.shape) > 2 else 256

    def add_vir(chain):
        rows = span(chain, 2 * width)

        @pl.loop(0, virtuals // piece)
        def _(t):
            new = lax.dot_general(
                amps[rows, span(t, piece)], amps[rows, :], contract, preferred_element_type=F32
            )
            where = span(t, vir.shape[0] * piece // virtuals)
            vir[where] += new.reshape((-1,) + vir.shape[1:])

    def add_three(chain):
        rows = span(chain, 2 * width)

        @pl.loop(0, 2 * nq)
        def _(t):
            three[t // 2, t % 2] += lax.dot_general(
                held[t // 2, t % 2, rows, :], amps[rows, :], contract, preferred_element_type=F32
            )

    def both(chain):
        absorb(2 * chain + low)
        arrived(2 * chain + 1 - low)
        absorb(2 * chain + 1 - low)

    @pl.loop(1, nz)
    def _(k):
        chain = nearest_first(z, k, nz)
        arrived(2 * chain + low)
        for d in range(1, nq):
            held_relay(d, chain, held_slot(d, 2 * chain + low), start)
        before = nearest_first(z, k - 1, nz)
        both(before)
        add_vir(before)
        add_three(before)

    last = nearest_first(z, nz - 1, nz)
    both(last)
    add_vir(last)
    vir_done()
    add_three(last)

    def finish():
        @pl.loop(0, nz)
        def _(chain):
            coef_relay(chain, coef_slot(2 * chain + low), sent)
            for d in range(1, nq):
                held_relay(d, chain, held_slot(d, 2 * chain + low), sent)

        @pl.loop(1, n)
        def _(d):
            block = (o + d) % n
            coef_across(block).wait_send()
            give(block, c).wait_send()

        for r in order:
            to_partner(r).wait_send()
            for d in range(1, nq):
                to_chip(d, r).wait_send()
                onward(d, r, c).wait_send()

    return finish


def reduction(
    n, nq, three, vir, near_out, far_out, vir_out,
    t_pair, t_out, t_far, v_pair, v_sum, v_side, v_line, v_chain, v_col, v_far,
    pair_send, pair_recv, t_send, t_recv, vp_send, vp_recv, x_send, x_recv, z_send, z_recv, y_send, y_recv,
):
    o = lax.axis_index("occ")
    s = lax.axis_index("aux")
    q, c = s // 2, s % 2
    z, low = o // 2, o % 2
    nz = n // 2
    chunks, chunk = v_pair.shape[0], v_pair.shape[-1]
    partner = (o, 2 * q + 1 - c)
    side = (2 * z + 1 - low, s)

    def cols(k):
        return pl.ds(k * chunk, chunk)

    def v_swap(k):
        return remote(vir.at[:, :, 1 - c, :, cols(k)], v_pair.at[k], vp_send.at[k], vp_recv.at[k], partner)

    def x_swap(k):
        return remote(v_sum.at[k, :, 1 - low], v_side.at[k], x_send.at[k], x_recv.at[k], side)

    def along(k, d):
        there = (z + d) % nz
        return remote(
            v_line.at[k, there], v_chain.at[k, d], z_send.at[k, d], z_recv.at[k, d], (2 * there + low, s)
        )

    def between(k, d):
        there = (q + d) % nq
        return remote(v_col.at[k, there], v_far.at[k, d], y_send.at[k, d], y_recv.at[k, d], (o, 2 * there + c))

    def swap(d):
        return remote(three.at[(q + d) % nq, 1 - c], t_pair.at[d], pair_send.at[d], pair_recv.at[d], partner)

    def spread(d):
        return remote(t_out.at[d], t_far.at[d], t_send.at[d], t_recv.at[d], (o, 2 * ((q + d) % nq) + c))

    order = list(range(1, nq)) + [0]

    def open_vir():
        for k in range(chunks):
            v_swap(k).start()

    def close():
        for d in order:
            swap(d).start()
        for k in range(chunks):
            v_swap(k).wait()
            v_sum[k] = (vir[:, :, c, :, cols(k)] + v_pair[k]).reshape(v_sum.shape[1:])
            x_swap(k).start()
        for d in order[:-1]:
            swap(d).wait()
            t_out[d] = three[(q + d) % nq, c] + t_pair[d]
            spread(d).start()
        for k in range(chunks):
            x_swap(k).wait()
            v_line[k] = v_sum[k, :, low] + v_side[k]
            for d in range(1, nz):
                along(k, d).start()
            if k == 0:
                swap(0).wait()
                near_out[...] = three[q, c] + t_pair[0]
        for k in range(chunks):
            held = v_line[k, z]
            for d in range(1, nz):
                along(k, d).wait()
                held += v_chain[k, d]
            v_col[k] = held
            for d in range(1, nq):
                between(k, d).start()
        for d in order[:-1]:
            spread(d).wait()
            far_out[...] = t_far[d] if d == 1 else far_out[...] + t_far[d]
        for k in range(chunks):
            rows = v_col[k, q]
            for d in range(1, nq):
                between(k, d).wait()
                rows += v_far[k, d]
            vir_out[:, cols(k)] = rows

    return open_vir, close


def amplitude_kernel(n, nq, *refs):
    make_densities(n, nq, *refs)()


def reduce_kernel(n, nq, *refs):
    greet(n, nq)()
    open_vir, close = reduction(n, nq, *refs)
    open_vir()
    close()


def whole_kernel(n, nq, inputs, outputs, count, *refs):
    operands, results, scratch = refs[:inputs], refs[inputs : inputs + outputs], refs[inputs + outputs :]
    three, vir, rest = scratch[0], scratch[1], scratch[2:]
    open_vir, close = reduction(n, nq, three, vir, *results, *rest[count:])
    finish = make_densities(n, nq, *operands, three, vir, *rest[:count], vir_done=open_vir)
    close()
    finish()


def per_device(half_integrals, vir_coef, occ_energy, vir_energy):
    n, aux = lax.axis_size("occ"), lax.axis_size("aux")
    nz, nq = n // 2, aux // 2
    _, tile, basis = half_integrals.shape
    part = vir_coef.shape[1]
    virtuals = part * n
    width, rows = virtuals // aux, virtuals // (n * aux)
    vmem = pl.BlockSpec(memory_space=pltpu.VMEM)
    dma = pltpu.SemaphoreType.DMA
    half = jnp.bfloat16
    lanes = 128
    chunks = virtuals // lanes

    def room(*shape):
        return pltpu.VMEM(shape, F32)

    def result(*shape):
        return jax.ShapeDtypeStruct(shape, F32)

    def call(kernel, name, number, in_specs, out_shape, scratch, operands):
        return pl.pallas_call(
            kernel,
            out_shape=out_shape,
            in_specs=in_specs,
            out_specs=(vmem,) * len(out_shape),
            scratch_shapes=scratch,
            compiler_params=pltpu.CompilerParams(
                collective_id=number, has_side_effects=True, vmem_limit_bytes=LIMIT
            ),
            name=name,
        )(*operands)

    operands = (occ_energy, half_integrals, vir_coef.T, vir_energy)
    specs = [pl.BlockSpec(memory_space=pltpu.SMEM), pl.BlockSpec(memory_space=pl.ANY), vmem, vmem]
    make_scratch = [
        pltpu.VMEM(half_integrals.shape, half),
        pltpu.VMEM((2, virtuals, basis // 2), half),
        pltpu.VMEM((nq, 2, nq, 2 * width, tile), half),
        pltpu.VMEM((nq, 2, n * width, tile), half),
        pltpu.VMEM((n, width, tile), half),
        pltpu.VMEM((n * width, virtuals), half),
        dma, dma((2,)), dma, dma((n,)), dma((nz,)), dma((nz,)), dma((nz,)), dma((n,)), dma((n,)),
        dma((nq, nq)), dma((nq, nq)), dma((nq, nq)), dma((nq, nq)), dma((nq,)), dma((nq,)), dma((n,)), dma((n,)),
        dma((nq, n)), dma((nq, nz)), dma((nq, nz)), dma((nq, nz)),
    ]
    reduce_scratch = [
        room(nq, tile, virtuals), room(nq, tile, virtuals), room(nq, tile, virtuals),
        room(chunks, n, nq, rows, lanes), room(chunks, nz, 2, nq, rows, lanes),
        room(chunks, nz, nq, rows, lanes), room(chunks, nz, nq, rows, lanes), room(chunks, nz, nq, rows, lanes),
        room(chunks, nq, rows, lanes), room(chunks, nq, rows, lanes),
        dma((nq,)), dma((nq,)), dma((nq,)), dma((nq,)), dma((chunks,)), dma((chunks,)), dma((chunks,)), dma((chunks,)),
        dma((chunks, nz)), dma((chunks, nz)), dma((chunks, nq)), dma((chunks, nq)),
    ]
    sums = (nq, 2, tile, virtuals)
    groups = (n, nq, 2, rows, virtuals)
    finals = (result(tile, virtuals), result(tile, virtuals), result(rows, virtuals))
    if rows % 8 == 0:
        kernel = functools.partial(whole_kernel, n, nq, len(specs), len(finals), len(make_scratch))
        scratch = [room(*sums), room(*groups)] + make_scratch + reduce_scratch
        near, far, vir_rows = call(kernel, "densities", 0, specs, finals, scratch, operands)
    else:
        kernel = functools.partial(amplitude_kernel, n, nq)
        partials = (result(*sums), result(virtuals, virtuals))
        three, vir = call(kernel, "amplitude", 0, specs, partials, make_scratch, operands)
        kernel = functools.partial(reduce_kernel, n, nq)
        near, far, vir_rows = call(
            kernel, "reduce", 1, [vmem, vmem], finals, reduce_scratch, (three, vir.reshape(groups))
        )
    return (near + far)[:, None, :], vir_rows / (n * virtuals)


def solution(mesh):
    return jax.shard_map(
        per_device,
        mesh=mesh,
        in_specs=(P(None, "aux", None), P(None, "occ"), P(), P()),
        out_specs=(P("aux", "occ", None), P(("occ", "aux"), None)),
        check_vma=False,
    )
```

profile of v0, /device:TPU:0, one launch (start us, length us, event | category | flops | bytes accessed | tf_op | source)
XLA Modules:
  0.0 89.2 jit_solution(14951842854237546676)
XLA Ops:
  0.6 83.9 %densities.1 = (f32[256,768]{1,0:T(8,128)}, f32[256,768]{1,0:T(8,128)}, f32[24,768]{1,0:T(8,128)}) custom-call(f32[8]{0:T(128)} %refs_0_.1, bf16[8,256,1024]{2,1,0:T(8,128)(2,1)} %refs_1_.1, bf16[96,1024]{1,0:T(8,128)(2,1)} %bitcast.3, f32[768]{0:T(1024)} %refs_3_.1), custom_call_target="tpu_custom_call" | custom-call | tf_op jit(solution)/shard_map/densities/pallas_call | solution.py:430
  84.5 1.5 %add_bitcast_fusion = f32[256,1,768]{2,0,1:T(8,128)S(1)} fusion(f32[256,768]{1,0:T(8,128)} %get-tuple-element.5, f32[256,768]{1,0:T(8,128)} %get-tuple-element.6), kind=kLoop, calls=%fused_computation | loop fusion | flops 196608 | bytes 2359296 | tf_op jit(solution)/shard_map/broadcast_in_dim | solution.py:478
  86.0 1.7 %copy.6 = f32[256,1,768]{2,1,0:T(1,128)} copy(f32[256,1,768]{2,0,1:T(8,128)S(1)} %add_bitcast_fusion) | data formatting | bytes 1572864
  87.7 1.5 %broadcast_multiply_fusion = f32[24,768]{1,0:T(8,128)} fusion(f32[24,768]{1,0:T(8,128)} %get-tuple-element.7), kind=kLoop, calls=%fused_computation.1 | loop fusion | flops 18432 | bytes 147456 | tf_op jit(solution)/shard_map/div | solution.py:478
where the time goes:
time: 89.4 us; the launch traced here: 89.2 us
  Pallas kernels  83.9 us (94%)
  other arithmetic  2.98 us (3%)
  local copies, waits for them, and re-layouts  1.69 us (2%)
    pallas_call x1, Pallas kernels, call(): pl.pallas_call(kernel, out_shape=out_shape, in_specs=in_specs, out_specs=...  83.9 us

commit v1 on v0

--- a/solution.py
+++ b/solution.py
@@ -407,12 +407,409 @@
     finish()
 
 
+def paired_kernel(
+    n, occ_e, half, coef, vir_e, three_out, vir_out,
+    ints, raw, full, own, held, gift, cross, amps, vir,
+    t_give, t_got, t_sum, t_far, n_give, n_got, v_pair, v_sum, v_side, v_line, v_chain, v_col, v_far,
+    i_sem, keep_sem, o_sem, raw_sems, c_recv, c_up, c_down, c_side, cp_send, cp_recv,
+    pn_sems, pf_sems, f_recv, f_send, z_fwd, x_fwd, y_send, g_send, g_recv,
+    t_sems, ts_sems, n_sems, vp_send, vp_recv, x_send, x_recv, z_send, z_recv, yv_send, yv_recv,
+):
+    o = lax.axis_index("occ")
+    s = lax.axis_index("aux")
+    q, c = s // 2, s % 2
+    z, low = o // 2, o % 2
+    nz = n // 2
+    far = 1 - q
+    part, basis = coef.shape
+    tile = raw.shape[0]
+    virtuals = full.shape[0]
+    width = virtuals // 4
+    piece = basis // 4
+    above, below, side = o + 2, o - 2, 2 * z + 1 - low
+    other = 2 * q + 1 - c
+    partner = (o, other)
+    opposite = (o, 2 * far + c)
+
+    def span(index, size):
+        return pl.ds(pl.multiple_of(index * size, size), size)
+
+    def start(copy):
+        copy.start()
+
+    def sent(copy):
+        copy.wait_send()
+
+    def nearest(k):
+        return nearest_first(z, k, nz)
+
+    barrier = pltpu.get_barrier_semaphore()
+    peers = [partner, opposite, (o, 2 * far + 1 - c), (side, s), (side, other)]
+    peers += [(2 * ((z + d) % nz) + low, t) for d in range(1, nz) for t in (s, other)]
+    for peer in peers:
+        pl.semaphore_signal(barrier, inc=1, device_id=peer, device_id_type=MESH)
+    fetch = pltpu.make_async_copy(half, ints, i_sem)
+    fetch.start()
+    keep = pltpu.make_async_copy(coef, full.at[span(o, part)], keep_sem)
+    keep.start()
+    pl.semaphore_wait(barrier, len(peers))
+
+    lend = remote(half.at[o], raw, raw_sems.at[0], raw_sems.at[1], opposite)
+    lend.start()
+
+    def coef_slot(block, core, h):
+        return full.at[span(block, part), pl.ds(pl.multiple_of((2 * core + h) * piece, piece), piece)]
+
+    def coef_relay(chain, h, src, act):
+        block = 2 * chain + low
+        dst = coef_slot(block, c, h)
+        recv = c_recv.at[block, h]
+        pl.when(jnp.logical_and(chain <= z, z < nz - 1))(
+            lambda: act(remote(src, dst, c_up.at[chain, h], recv, (above, s)))
+        )
+        pl.when(jnp.logical_and(chain >= z, z > 0))(
+            lambda: act(remote(src, dst, c_down.at[chain, h], recv, (below, s)))
+        )
+        act(remote(src, dst, c_side.at[chain, h], recv, (side, s)))
+
+    def coef_across(block, h, core):
+        ref = coef_slot(block, core, h)
+        return remote(ref, ref, cp_send.at[block, h], cp_recv.at[block, h], partner)
+
+    def coef_wait(block, h):
+        ref = coef_slot(block, c, h)
+        remote(ref, ref, c_side.at[0, h], c_recv.at[block, h], (side, s)).wait_recv()
+
+    for h in range(2):
+        coef_relay(z, h, coef.at[:, pl.ds(pl.multiple_of((2 * c + h) * piece, piece), piece)], start)
+    row_e = vir_e[...].reshape(1, virtuals)
+    here = lax.broadcasted_iota(jnp.int32, (width, virtuals), 0) + s * width
+    there = lax.broadcasted_iota(jnp.int32, (width, virtuals), 1)
+    col_e = jnp.sum(jnp.where(here == there, row_e, 0.0), axis=1, keepdims=True)
+
+    def coef_beside(k):
+        block = 2 * nearest(k) + 1 - low
+        for h in range(2):
+            coef_wait(block, h)
+            coef_across(block, h, c).start()
+
+    @pl.loop(1, nz)
+    def _(k):
+        chain = nearest(k)
+        block = 2 * chain + low
+        for h in range(2):
+            coef_wait(block, h)
+            coef_relay(chain, h, coef_slot(block, c, h), start)
+            coef_across(block, h, c).start()
+        coef_beside(k - 1)
+
+    coef_beside(nz - 1)
+
+    @pl.loop(1, n)
+    def _(d):
+        block = (o + d) % n
+        for h in range(2):
+            coef_across(block, h, 1 - c).wait_recv()
+
+    keep.wait()
+    fetch.wait()
+
+    def transform(rows, source):
+        return lax.dot_general(rows, source, (((1,), (1,)), ((), ())), preferred_element_type=F32).astype(jnp.bfloat16)
+
+    def cols(group, core):
+        return span(2 * group + core, tile)
+
+    def lend_block(block, act):
+        for core in range(2):
+            act(
+                remote(
+                    cross.at[block, pl.ds(core * width, width)], held.at[span(block, width), cols(q, c)],
+                    y_send.at[block, core], f_recv.at[block, c], (o, 2 * far + core),
+                )
+            )
+
+    def distant(chain):
+        return jnp.abs(chain - z) > 2
+
+    def lend_blocks(k, act):
+        chain = nearest(k)
+        act(2 * chain + 1 - low)
+        pl.when(distant(chain))(lambda: act(2 * chain + low))
+
+    def cross_over(block):
+        cross[block] = transform(full[span(far, 2 * width), :], ints[block])
+        lend_block(block, start)
+
+    @pl.loop(2, nz)
+    def _(k):
+        lend_blocks(k, cross_over)
+
+    def own_part(group, core):
+        return own.at[:, cols(group, core)]
+
+    def near_part(core):
+        ref = own_part(q, core)
+        return remote(ref, ref, pn_sems.at[0], pn_sems.at[1], partner)
+
+    def far_part(core):
+        ref = own_part(far, core)
+        return remote(ref, ref, pf_sems.at[0], pf_sems.at[1], partner)
+
+    def hand_out(act):
+        for core in range(2):
+            src = own.at[span(2 * q + core, width), cols(far, c)]
+            dst = held.at[span(o, width), cols(far, c)]
+            recv = f_recv.at[o, c]
+            pl.when(z < nz - 1)(lambda: act(remote(src, dst, f_send.at[0, core], recv, (above, 2 * q + core))))
+            pl.when(z > 0)(lambda: act(remote(src, dst, f_send.at[1, core], recv, (below, 2 * q + core))))
+        for core in range(2):
+            src = own.at[span(2 * q + core, width), cols(far, c)]
+            dst = held.at[span(o, width), cols(far, c)]
+            act(remote(src, dst, f_send.at[2, core], f_recv.at[o, c], (side, 2 * q + core)))
+
+    lend.wait_recv()
+    own[:, cols(far, c)] = transform(full[...], raw[...])
+    hand_out(start)
+    far_part(c).start()
+    own[:, cols(q, c)] = transform(full[...], ints[o])
+    near_part(c).start()
+
+    def give(block, core):
+        return remote(
+            gift.at[block], held.at[span(block, width), cols(q, core)], g_send.at[block], g_recv.at[block], partner
+        )
+
+    @pl.loop(1, n)
+    def _(d):
+        block = (o + d) % n
+        rows = jnp.concatenate([full[span(s, width), :], full[span(other, width), :]], axis=0)
+        both = transform(rows, ints[block])
+        held[span(block, width), cols(q, c)] = both[:width]
+        gift[block] = both[width:]
+        give(block, c).start()
+
+    far_part(1 - c).wait_recv()
+    near_part(1 - c).wait_recv()
+    mine = pltpu.make_async_copy(own.at[span(s, width)], held.at[span(o, width)], o_sem)
+    mine.start()
+
+    def far_slot(block, core):
+        return held.at[span(block, width), cols(far, core)]
+
+    def arrive(block):
+        for core in range(2):
+            ref = far_slot(block, core)
+            remote(ref, ref, x_fwd.at[0], f_recv.at[block, core], (side, s)).wait_recv()
+
+    def pass_on(chain, act):
+        block = 2 * chain + low
+        for core in range(2):
+            ref = far_slot(block, core)
+            recv = f_recv.at[block, core]
+            pl.when(jnp.logical_and(chain < z, z < nz - 1))(
+                lambda: act(remote(ref, ref, z_fwd.at[0, core], recv, (above, s)))
+            )
+            pl.when(jnp.logical_and(chain > z, z > 0))(
+                lambda: act(remote(ref, ref, z_fwd.at[1, core], recv, (below, s)))
+            )
+            pl.when(chain == nearest(1))(lambda: act(remote(ref, ref, x_fwd.at[core], recv, (side, s))))
+
+    def beside_each(act):
+        pl.when(z > 0)(lambda: act(z - 1))
+        pl.when(z < nz - 1)(lambda: act(z + 1))
+
+    def take(chain):
+        arrive(2 * chain + low)
+        pass_on(chain, start)
+
+    beside_each(take)
+    mine.wait()
+
+    def absorb(chain):
+        rows = span(chain, 2 * width)
+        coulomb = lax.dot_general(
+            held[rows, :], own[...], (((1,), (1,)), ((), ())), preferred_element_type=F32
+        )
+        left = jnp.concatenate([occ_e[o] + occ_e[2 * chain + t] - col_e for t in range(2)], axis=0)
+        amps[rows, :] = (coulomb / (left - row_e)).astype(jnp.bfloat16)
+
+    @pl.loop(0, nz)
+    def _(k):
+        chain = nearest(k)
+        pl.when(jnp.abs(chain - z) > 1)(lambda: arrive(2 * chain + low))
+        arrive(2 * chain + 1 - low)
+        pl.when(chain != z)(lambda: give(2 * chain + low, 1 - c).wait_recv())
+        give(2 * chain + 1 - low, 1 - c).wait_recv()
+        absorb(chain)
+
+    contract = (((0,), (0,)), ((), ()))
+    strips, strip = t_give.shape[0], t_give.shape[-1]
+    chunks, chunk = v_pair.shape[0], v_pair.shape[-1]
+
+    def lanes(k):
+        return pl.ds(k * chunk, chunk)
+
+    def wide(k):
+        return pl.ds(k * strip, strip)
+
+    def part_three(group, core, where):
+        return lax.dot_general(
+            held[:, cols(group, core)], amps[:, where], contract, preferred_element_type=F32
+        )
+
+    def far_swap(k):
+        return remote(t_give.at[k], t_got.at[k], t_sems.at[0, k], t_sems.at[1, k], partner)
+
+    def far_send(k):
+        return remote(t_sum.at[k], t_far.at[k], ts_sems.at[0, k], ts_sems.at[1, k], opposite)
+
+    def v_swap(k):
+        return remote(vir.at[:, :, 1 - c, :, lanes(k)], v_pair.at[k], vp_send.at[k], vp_recv.at[k], partner)
+
+    def x_swap(k):
+        return remote(v_sum.at[k, :, 1 - low], v_side.at[k], x_send.at[k], x_recv.at[k], (side, s))
+
+    def along(k, d):
+        to = (z + d) % nz
+        return remote(v_line.at[k, to], v_chain.at[k, d], z_send.at[k, d], z_recv.at[k, d], (2 * to + low, s))
+
+    def between(k):
+        return remote(v_col.at[k, far], v_far.at[k], yv_send.at[k], yv_recv.at[k], opposite)
+
+    near_swap = remote(n_give, n_got, n_sems.at[0], n_sems.at[1], partner)
+    for k in range(strips):
+        t_give[k] = part_three(far, 1 - c, wide(k))
+        far_swap(k).start()
+    for k in range(strips):
+        t_sum[k] = part_three(far, c, wide(k))
+        far_swap(k).wait_recv()
+        t_sum[k] += t_got[k]
+        far_send(k).start()
+    for k in range(strips):
+        new = lax.dot_general(amps[...], amps[:, wide(k)], contract, preferred_element_type=F32)
+        vir[:, :, :, :, wide(k)] = new.reshape(vir.shape[:-1] + (strip,))
+        for t in range(k * strip // chunk, (k + 1) * strip // chunk):
+            v_swap(t).start()
+    n_give[...] = part_three(q, 1 - c, slice(None))
+    near_swap.start()
+    for k in range(chunks):
+        v_swap(k).wait_recv()
+        v_sum[k] = (vir[:, :, c, :, lanes(k)] + v_pair[k]).reshape(v_sum.shape[1:])
+        x_swap(k).start()
+    three_out[...] = part_three(q, c, slice(None))
+    for k in range(chunks):
+        x_swap(k).wait_recv()
+        v_line[k] = v_sum[k, :, low] + v_side[k]
+        for d in range(1, nz):
+            along(k, d).start()
+    near_swap.wait_recv()
+    three_out[...] += n_got[...]
+    for k in range(chunks):
+        total = v_line[k, z]
+        for d in range(1, nz):
+            along(k, d).wait_recv()
+            total += v_chain[k, d]
+        v_col[k] = total
+        between(k).start()
+    for k in range(strips):
+        far_send(k).wait_recv()
+        three_out[:, wide(k)] += t_far[k]
+    for k in range(chunks):
+        between(k).wait_recv()
+        vir_out[:, lanes(k)] = (v_col[k, q] + v_far[k]) / (n * virtuals)
+
+    lend.wait_send()
+
+    @pl.loop(0, nz)
+    def _(chain):
+        for h in range(2):
+            coef_relay(chain, h, coef_slot(2 * chain + low, c, h), sent)
+
+    @pl.loop(1, n)
+    def _(d):
+        block = (o + d) % n
+        for h in range(2):
+            coef_across(block, h, c).wait_send()
+        give(block, c).wait_send()
+
+    @pl.loop(2, nz)
+    def _(k):
+        lend_blocks(k, lambda block: lend_block(block, sent))
+
+    hand_out(sent)
+    far_part(c).wait_send()
+    near_part(c).wait_send()
+    beside_each(lambda chain: pass_on(chain, sent))
+    near_swap.wait_send()
+    for k in range(strips):
+        far_swap(k).wait_send()
+        far_send(k).wait_send()
+    for k in range(chunks):
+        v_swap(k).wait_send()
+        x_swap(k).wait_send()
+        between(k).wait_send()
+        for d in range(1, nz):
+            along(k, d).wait_send()
+
+
+def paired(n, half_integrals, coef, occ_energy, vir_energy):
+    _, tile, basis = half_integrals.shape
+    part = coef.shape[0]
+    virtuals = part * n
+    width, rows, nz = virtuals // 4, virtuals // (4 * n), n // 2
+    vmem = pl.BlockSpec(memory_space=pltpu.VMEM)
+    dma = pltpu.SemaphoreType.DMA
+    lanes = 128
+    chunks = virtuals // lanes
+    strip = 2 * lanes if chunks % 2 == 0 else lanes
+    strips = virtuals // strip
+
+    def room(*shape):
+        return pltpu.VMEM(shape, F32)
+
+    def packed(*shape):
+        return pltpu.VMEM(shape, jnp.bfloat16)
+
+    scratch = [
+        packed(n, tile, basis), packed(tile, basis), packed(virtuals, basis), packed(virtuals, 4 * tile),
+        packed(n * width, 4 * tile), packed(n, width, tile), packed(n, 2 * width, tile), packed(n * width, virtuals),
+        room(n, 2, 2, rows, virtuals),
+        room(strips, tile, strip), room(strips, tile, strip), room(strips, tile, strip), room(strips, tile, strip),
+        room(tile, virtuals), room(tile, virtuals),
+        room(chunks, n, 2, rows, lanes), room(chunks, nz, 2, 2, rows, lanes), room(chunks, nz, 2, rows, lanes),
+        room(chunks, nz, 2, rows, lanes), room(chunks, nz, 2, rows, lanes), room(chunks, 2, rows, lanes),
+        room(chunks, rows, lanes),
+        dma, dma, dma, dma((2,)), dma((n, 2)), dma((nz, 2)), dma((nz, 2)), dma((nz, 2)), dma((n, 2)), dma((n, 2)),
+        dma((2,)), dma((2,)), dma((n, 2)), dma((3, 2)), dma((2, 2)), dma((2,)), dma((n, 2)), dma((n,)), dma((n,)),
+        dma((2, strips)), dma((2, strips)), dma((2,)),
+        dma((chunks,)), dma((chunks,)), dma((chunks,)), dma((chunks,)), dma((chunks, nz)), dma((chunks, nz)),
+        dma((chunks,)), dma((chunks,)),
+    ]
+    return pl.pallas_call(
+        functools.partial(paired_kernel, n),
+        out_shape=(
+            jax.ShapeDtypeStruct((tile, virtuals), F32), jax.ShapeDtypeStruct((rows, virtuals), F32),
+        ),
+        in_specs=[pl.BlockSpec(memory_space=pltpu.SMEM), pl.BlockSpec(memory_space=pl.ANY), vmem, vmem],
+        out_specs=(vmem, vmem),
+        scratch_shapes=scratch,
+        compiler_params=pltpu.CompilerParams(
+            collective_id=0, has_side_effects=True, vmem_limit_bytes=LIMIT
+        ),
+        name="densities",
+    )(occ_energy, half_integrals, coef, vir_energy)
+
+
 def per_device(half_integrals, vir_coef, occ_energy, vir_energy):
     n, aux = lax.axis_size("occ"), lax.axis_size("aux")
     nz, nq = n // 2, aux // 2
     _, tile, basis = half_integrals.shape
     part = vir_coef.shape[1]
     virtuals = part * n
+    if nq == 2 and n % 2 == 0 and nz > 1 and virtuals % (32 * n) == 0 and virtuals % 128 == 0:
+        three, vir_rows = paired(n, half_integrals, vir_coef.T, occ_energy, vir_energy)
+        return three[:, None, :], vir_rows
     width, rows = virtuals // aux, virtuals // (n * aux)
     vmem = pl.BlockSpec(memory_space=pltpu.VMEM)
     dma = pltpu.SemaphoreType.DMA

time: 89.4 us -> 76.5 us (0.86)
  Pallas kernels: 83.9 us -> 71.3 us
  other arithmetic: 2.98 us -> 0 us
  local copies, waits for them, and re-layouts: 1.69 us -> 4.34 us
    pallas_call x1, Pallas kernels: 83.9 us -> 71.3 us  [paired(): pl.pallas_call(functools.partial(paired_kernel, n), out_shape=(jax.ShapeD...]
    unnamed x1 -> x2, local copies, waits for them, and re-layouts: 1.69 us -> 4.34 us
    div x1 -> x0, other arithmetic: 1.52 us -> none  [per_device(): return ((near + far)[:, None, :], vir_rows / (n * virtuals))]
    broadcast_in_dim x1 -> x0, other arithmetic: 1.46 us -> none  [per_device(): return ((near + far)[:, None, :], vir_rows / (n * virtuals))]
where the time goes in v1:
time: 76.5 us; the launch traced here: 76.2 us
  Pallas kernels  71.3 us (93%)
  local copies, waits for them, and re-layouts  4.34 us (6%)
    pallas_call x1, Pallas kernels, paired(): pl.pallas_call(functools.partial(paired_kernel, n), out_shape=(jax.ShapeD...  71.3 us
    unnamed x2, local copies, waits for them, and re-layouts  4.34 us

profile of v1, /device:TPU:0, one launch (start us, length us, event | category | flops | bytes accessed | tf_op | source)
XLA Modules:
  0.0 76.2 jit_solution(4800047137091023505)
XLA Ops:
  0.6 71.3 %densities.1 = (f32[256,768]{1,0:T(8,128)}, f32[24,768]{1,0:T(8,128)}) custom-call(f32[8]{0:T(128)} %occ_e.1, bf16[8,256,1024]{2,1,0:T(8,128)(2,1)} %half.1, bf16[96,1024]{1,0:T(8,128)(2,1)} %bitcast.3, f32[768]{0:T(1024)} %vir_e.1), custom_call_target="tpu_custom_call" | custom-call | tf_op jit(solution)/shard_map/densities/pallas_call | solution.py:789
  71.9 2.8 %copy.6 = f32[256,1,768]{2,1,0:T(1,128)} copy(f32[256,1,768]{2,0,1:T(8,128)} %bitcast.2) | data formatting | bytes 1572864
  74.7 1.5 %copy.8 = f32[24,768]{1,0:T(8,128)} copy(f32[24,768]{1,0:T(8,128)} %get-tuple-element.11) | data formatting | bytes 147456

commit v2 on v1

--- a/solution.py
+++ b/solution.py
@@ -9,6 +9,9 @@
 
 MESH = pl.DeviceIdType.MESH
 F32 = jnp.float32
+PIECES = 4
+SPAN = 80.0
+TINY = 1e-30
 LIMIT = 56 * 1024 * 1024
 
 
@@ -410,10 +413,12 @@
 def paired_kernel(
     n, occ_e, half, coef, vir_e, three_out, vir_out,
     ints, raw, full, own, held, gift, cross, amps, vir,
-    t_give, t_got, t_sum, t_far, n_give, n_got, v_pair, v_sum, v_side, v_line, v_chain, v_col, v_far,
+    t_give, t_got, n_give, n_got, v_pair, v_line, v_col, v_far,
+    t_code, t_scale, t_code_in, t_scale_in, x_code, x_scale, x_code_in, x_scale_in,
+    z_code, z_scale, z_code_in, z_scale_in,
     i_sem, keep_sem, o_sem, raw_sems, c_recv, c_up, c_down, c_side, cp_send, cp_recv,
     pn_sems, pf_sems, f_recv, f_send, z_fwd, x_fwd, y_send, g_send, g_recv,
-    t_sems, ts_sems, n_sems, vp_send, vp_recv, x_send, x_recv, z_send, z_recv, yv_send, yv_recv,
+    t_sems, ts_send, ts_recv, n_sems, vp_send, vp_recv, x_send, x_recv, z_send, z_recv, yv_send, yv_recv,
 ):
     o = lax.axis_index("occ")
     s = lax.axis_index("aux")
@@ -425,7 +430,8 @@
     tile = raw.shape[0]
     virtuals = full.shape[0]
     width = virtuals // 4
-    piece = basis // 4
+    pieces = c_recv.shape[1]
+    piece = basis // (2 * pieces)
     above, below, side = o + 2, o - 2, 2 * z + 1 - low
     other = 2 * q + 1 - c
     partner = (o, other)
@@ -458,7 +464,7 @@
     lend.start()
 
     def coef_slot(block, core, h):
-        return full.at[span(block, part), pl.ds(pl.multiple_of((2 * core + h) * piece, piece), piece)]
+        return full.at[span(block, part), pl.ds(pl.multiple_of((pieces * core + h) * piece, piece), piece)]
 
     def coef_relay(chain, h, src, act):
         block = 2 * chain + low
@@ -480,8 +486,8 @@
         ref = coef_slot(block, c, h)
         remote(ref, ref, c_side.at[0, h], c_recv.at[block, h], (side, s)).wait_recv()
 
-    for h in range(2):
-        coef_relay(z, h, coef.at[:, pl.ds(pl.multiple_of((2 * c + h) * piece, piece), piece)], start)
+    for h in range(pieces):
+        coef_relay(z, h, coef.at[:, pl.ds(pl.multiple_of((pieces * c + h) * piece, piece), piece)], start)
     row_e = vir_e[...].reshape(1, virtuals)
     here = lax.broadcasted_iota(jnp.int32, (width, virtuals), 0) + s * width
     there = lax.broadcasted_iota(jnp.int32, (width, virtuals), 1)
@@ -489,7 +495,7 @@
 
     def coef_beside(k):
         block = 2 * nearest(k) + 1 - low
-        for h in range(2):
+        for h in range(pieces):
             coef_wait(block, h)
             coef_across(block, h, c).start()
 
@@ -497,7 +503,7 @@
     def _(k):
         chain = nearest(k)
         block = 2 * chain + low
-        for h in range(2):
+        for h in range(pieces):
             coef_wait(block, h)
             coef_relay(chain, h, coef_slot(block, c, h), start)
             coef_across(block, h, c).start()
@@ -508,7 +514,7 @@
     @pl.loop(1, n)
     def _(d):
         block = (o + d) % n
-        for h in range(2):
+        for h in range(pieces):
             coef_across(block, h, 1 - c).wait_recv()
 
     keep.wait()
@@ -635,8 +641,8 @@
         amps[rows, :] = (coulomb / (left - row_e)).astype(jnp.bfloat16)
 
     @pl.loop(0, nz)
-    def _(k):
-        chain = nearest(k)
+    def _(i):
+        chain = nearest(jnp.where(i == 0, 0, jnp.where(i == nz - 1, 1, i + 1)))
         pl.when(jnp.abs(chain - z) > 1)(lambda: arrive(2 * chain + low))
         arrive(2 * chain + 1 - low)
         pl.when(chain != z)(lambda: give(2 * chain + low, 1 - c).wait_recv())
@@ -645,10 +651,8 @@
 
     contract = (((0,), (0,)), ((), ()))
     strips, strip = t_give.shape[0], t_give.shape[-1]
-    chunks, chunk = v_pair.shape[0], v_pair.shape[-1]
-
-    def lanes(k):
-        return pl.ds(k * chunk, chunk)
+    rows = vir.shape[4]
+    middle = virtuals // 2
 
     def wide(k):
         return pl.ds(k * strip, strip)
@@ -661,75 +665,125 @@
     def far_swap(k):
         return remote(t_give.at[k], t_got.at[k], t_sems.at[0, k], t_sems.at[1, k], partner)
 
+    def coded_copies(code, scale, code_to, scale_to, sems, target):
+        return (
+            remote(code, code_to, sems[0].at[0], sems[1].at[0], target),
+            remote(scale, scale_to, sems[0].at[1], sems[1].at[1], target),
+        )
+
     def far_send(k):
-        return remote(t_sum.at[k], t_far.at[k], ts_sems.at[0, k], ts_sems.at[1, k], opposite)
-
-    def v_swap(k):
-        return remote(vir.at[:, :, 1 - c, :, lanes(k)], v_pair.at[k], vp_send.at[k], vp_recv.at[k], partner)
-
-    def x_swap(k):
-        return remote(v_sum.at[k, :, 1 - low], v_side.at[k], x_send.at[k], x_recv.at[k], (side, s))
-
-    def along(k, d):
-        to = (z + d) % nz
-        return remote(v_line.at[k, to], v_chain.at[k, d], z_send.at[k, d], z_recv.at[k, d], (2 * to + low, s))
-
-    def between(k):
-        return remote(v_col.at[k, far], v_far.at[k], yv_send.at[k], yv_recv.at[k], opposite)
+        sems = (ts_send.at[k], ts_recv.at[k])
+        return coded_copies(t_code.at[k], t_scale.at[k], t_code_in.at[k], t_scale_in.at[k], sems, opposite)
+
+    def x_swap(chain):
+        sems = (x_send.at[chain], x_recv.at[chain])
+        return coded_copies(
+            x_code.at[chain], x_scale.at[chain], x_code_in.at[chain], x_scale_in.at[chain], sems, (side, s)
+        )
+
+    def along(to, sender):
+        sems = (z_send.at[to], z_recv.at[sender])
+        return coded_copies(
+            z_code.at[to], z_scale.at[to], z_code_in.at[sender], z_scale_in.at[sender], sems, (2 * to + low, s)
+        )
+
+    def both_start(copies):
+        for copy in copies:
+            copy.start()
+
+    def both_recv(copies):
+        for copy in copies:
+            copy.wait_recv()
+
+    def both_sent(copies):
+        for copy in copies:
+            copy.wait_send()
+
+    def encode(value, code, scale):
+        parts = scale.shape[0]
+        size = value.shape[0] // parts
+        grouped = value.reshape(parts, size, value.shape[1])
+        top = jnp.maximum(jnp.max(jnp.abs(grouped), axis=1, keepdims=True), TINY)
+        scale[...] = top
+        code[...] = jnp.exp(grouped * (SPAN / top)).astype(jnp.bfloat16).reshape(value.shape)
+
+    def decode(code, scale):
+        parts = scale.shape[0]
+        words = jnp.log(code[...].astype(F32)).reshape(parts, code.shape[0] // parts, code.shape[1])
+        return (words * (scale[...] * (1.0 / SPAN))).reshape(code.shape)
+
+    def v_swap(chain):
+        return remote(vir.at[chain, :, :, 1 - c], v_pair.at[chain], vp_send.at[chain], vp_recv.at[chain], partner)
+
+    def between():
+        return remote(v_col.at[far], v_far, yv_send, yv_recv, opposite)
 
     near_swap = remote(n_give, n_got, n_sems.at[0], n_sems.at[1], partner)
+    first = jnp.where(z < nz // 2, 1, 0)
+    for half in (first, 1 - first):
+        new = lax.dot_general(
+            amps[:, span(half, middle)], amps[...], contract, preferred_element_type=F32
+        )
+        vir[pl.ds(half * (nz // 2), nz // 2)] = new.reshape((nz // 2,) + vir.shape[1:])
+        for t in range(nz // 2):
+            v_swap(half * (nz // 2) + t).start()
+
+    def pair_sum(chain, across):
+        return (vir[chain, across, :, c] + v_pair[chain, across]).reshape(2 * rows, virtuals)
+
+    farthest = [nearest(k) for k in reversed(range(nz))]
+
+    def add_pair(chain):
+        v_swap(chain).wait_recv()
+        encode(pair_sum(chain, 1 - low), x_code.at[chain], x_scale.at[chain])
+        both_start(x_swap(chain))
+
+    for k in range(max(strips, nz)):
+        if k < strips:
+            t_give[k] = part_three(far, 1 - c, wide(k))
+            far_swap(k).start()
+        if k < nz:
+            add_pair(farthest[k])
     for k in range(strips):
-        t_give[k] = part_three(far, 1 - c, wide(k))
-        far_swap(k).start()
-    for k in range(strips):
-        t_sum[k] = part_three(far, c, wide(k))
+        new = part_three(far, c, wide(k))
         far_swap(k).wait_recv()
-        t_sum[k] += t_got[k]
-        far_send(k).start()
-    for k in range(strips):
-        new = lax.dot_general(amps[...], amps[:, wide(k)], contract, preferred_element_type=F32)
-        vir[:, :, :, :, wide(k)] = new.reshape(vir.shape[:-1] + (strip,))
-        for t in range(k * strip // chunk, (k + 1) * strip // chunk):
-            v_swap(t).start()
+        encode(new + t_got[k], t_code.at[k], t_scale.at[k])
+        both_start(far_send(k))
     n_give[...] = part_three(q, 1 - c, slice(None))
     near_swap.start()
-    for k in range(chunks):
-        v_swap(k).wait_recv()
-        v_sum[k] = (vir[:, :, c, :, lanes(k)] + v_pair[k]).reshape(v_sum.shape[1:])
-        x_swap(k).start()
     three_out[...] = part_three(q, c, slice(None))
-    for k in range(chunks):
-        x_swap(k).wait_recv()
-        v_line[k] = v_sum[k, :, low] + v_side[k]
-        for d in range(1, nz):
-            along(k, d).start()
+    for chain in farthest:
+        both_recv(x_swap(chain))
+        total = pair_sum(chain, low) + decode(x_code_in.at[chain], x_scale_in.at[chain])
+        v_line[...] = total
+        if chain is not farthest[-1]:
+            encode(total, z_code.at[chain], z_scale.at[chain])
+            both_start(along(chain, z))
     near_swap.wait_recv()
     three_out[...] += n_got[...]
-    for k in range(chunks):
-        total = v_line[k, z]
-        for d in range(1, nz):
-            along(k, d).wait_recv()
-            total += v_chain[k, d]
-        v_col[k] = total
-        between(k).start()
+    for k in range(1, nz):
+        sender = nearest(k)
+        both_recv(along(sender, sender))
+        v_line[...] += decode(z_code_in.at[sender], z_scale_in.at[sender])
+    v_col[...] = v_line[...].reshape(v_col.shape)
+    between().start()
     for k in range(strips):
-        far_send(k).wait_recv()
-        three_out[:, wide(k)] += t_far[k]
-    for k in range(chunks):
-        between(k).wait_recv()
-        vir_out[:, lanes(k)] = (v_col[k, q] + v_far[k]) / (n * virtuals)
+        both_recv(far_send(k))
+        three_out[:, wide(k)] += decode(t_code_in.at[k], t_scale_in.at[k])
+    between().wait_recv()
+    vir_out[...] = (v_col[q] + v_far[...]) / (n * virtuals)
 
     lend.wait_send()
 
     @pl.loop(0, nz)
     def _(chain):
-        for h in range(2):
+        for h in range(pieces):
             coef_relay(chain, h, coef_slot(2 * chain + low, c, h), sent)
 
     @pl.loop(1, n)
     def _(d):
         block = (o + d) % n
-        for h in range(2):
+        for h in range(pieces):
             coef_across(block, h, c).wait_send()
         give(block, c).wait_send()
 
@@ -744,13 +798,13 @@
     near_swap.wait_send()
     for k in range(strips):
         far_swap(k).wait_send()
-        far_send(k).wait_send()
-    for k in range(chunks):
-        v_swap(k).wait_send()
-        x_swap(k).wait_send()
-        between(k).wait_send()
-        for d in range(1, nz):
-            along(k, d).wait_send()
+        both_sent(far_send(k))
+    for chain in range(nz):
+        v_swap(chain).wait_send()
+        both_sent(x_swap(chain))
+    for k in range(1, nz):
+        both_sent(along(nearest(k), z))
+    between().wait_send()
 
 
 def paired(n, half_integrals, coef, occ_energy, vir_energy):
@@ -758,6 +812,7 @@
     part = coef.shape[0]
     virtuals = part * n
     width, rows, nz = virtuals // 4, virtuals // (4 * n), n // 2
+    pieces = PIECES if basis % (256 * PIECES) == 0 else 1
     vmem = pl.BlockSpec(memory_space=pltpu.VMEM)
     dma = pltpu.SemaphoreType.DMA
     lanes = 128
@@ -774,17 +829,21 @@
     scratch = [
         packed(n, tile, basis), packed(tile, basis), packed(virtuals, basis), packed(virtuals, 4 * tile),
         packed(n * width, 4 * tile), packed(n, width, tile), packed(n, 2 * width, tile), packed(n * width, virtuals),
-        room(n, 2, 2, rows, virtuals),
-        room(strips, tile, strip), room(strips, tile, strip), room(strips, tile, strip), room(strips, tile, strip),
-        room(tile, virtuals), room(tile, virtuals),
-        room(chunks, n, 2, rows, lanes), room(chunks, nz, 2, 2, rows, lanes), room(chunks, nz, 2, rows, lanes),
-        room(chunks, nz, 2, rows, lanes), room(chunks, nz, 2, rows, lanes), room(chunks, 2, rows, lanes),
-        room(chunks, rows, lanes),
-        dma, dma, dma, dma((2,)), dma((n, 2)), dma((nz, 2)), dma((nz, 2)), dma((nz, 2)), dma((n, 2)), dma((n, 2)),
+        room(nz, 2, 2, 2, rows, virtuals),
+        room(strips, tile, strip), room(strips, tile, strip), room(tile, virtuals), room(tile, virtuals),
+        room(nz, 2, 2, rows, virtuals), room(2 * rows, virtuals), room(2, rows, virtuals), room(rows, virtuals),
+    ]
+    groups = tile // 32
+    for _ in range(2):
+        scratch += [packed(strips, tile, strip), room(strips, groups, 1, strip)]
+    for _ in range(4):
+        scratch += [packed(nz, 2 * rows, virtuals), room(nz, 2, 1, virtuals)]
+    scratch += [
+        dma, dma, dma, dma((2,)), dma((n, pieces)), dma((nz, pieces)), dma((nz, pieces)), dma((nz, pieces)),
+        dma((n, pieces)), dma((n, pieces)),
         dma((2,)), dma((2,)), dma((n, 2)), dma((3, 2)), dma((2, 2)), dma((2,)), dma((n, 2)), dma((n,)), dma((n,)),
-        dma((2, strips)), dma((2, strips)), dma((2,)),
-        dma((chunks,)), dma((chunks,)), dma((chunks,)), dma((chunks,)), dma((chunks, nz)), dma((chunks, nz)),
-        dma((chunks,)), dma((chunks,)),
+        dma((2, strips)), dma((strips, 2)), dma((strips, 2)), dma((2,)),
+        dma((nz,)), dma((nz,)), dma((nz, 2)), dma((nz, 2)), dma((nz, 2)), dma((nz, 2)), dma, dma,
     ]
     return pl.pallas_call(
         functools.partial(paired_kernel, n),
@@ -807,7 +866,7 @@
     _, tile, basis = half_integrals.shape
     part = vir_coef.shape[1]
     virtuals = part * n
-    if nq == 2 and n % 2 == 0 and nz > 1 and virtuals % (32 * n) == 0 and virtuals % 128 == 0:
+    if nq == 2 and n % 2 == 0 and nz > 1 and nz % 2 == 0 and virtuals % (32 * n) == 0 and virtuals % 256 == 0 and tile % 32 == 0:
         three, vir_rows = paired(n, half_integrals, vir_coef.T, occ_energy, vir_energy)
         return three[:, None, :], vir_rows
     width, rows = virtuals // aux, virtuals // (n * aux)

time: 76.5 us -> 64.8 us (0.85)
  Pallas kernels: 71.3 us -> 59.6 us
    pallas_call x1, Pallas kernels: 71.3 us -> 59.6 us  [paired(): pl.pallas_call(functools.partial(paired_kernel, n), out_shape=(jax.ShapeD...]
where the time goes in v2:
time: 64.8 us; the launch traced here: 64.6 us
  Pallas kernels  59.6 us (92%)
  local copies, waits for them, and re-layouts  4.34 us (7%)
    pallas_call x1, Pallas kernels, paired(): pl.pallas_call(functools.partial(paired_kernel, n), out_shape=(jax.ShapeD...  59.6 us
    unnamed x2, local copies, waits for them, and re-layouts  4.34 us

profile of v2, /device:TPU:0, one launch (start us, length us, event | category | flops | bytes accessed | tf_op | source)
XLA Modules:
  0.0 64.6 jit_solution(10087171842379259114)
XLA Ops:
  0.6 59.6 %densities.1 = (f32[256,768]{1,0:T(8,128)}, f32[24,768]{1,0:T(8,128)}) custom-call(f32[8]{0:T(128)} %occ_e.1, bf16[8,256,1024]{2,1,0:T(8,128)(2,1)} %half.1, bf16[96,1024]{1,0:T(8,128)(2,1)} %bitcast.3, f32[768]{0:T(1024)} %vir_e.1), custom_call_target="tpu_custom_call" | custom-call | tf_op jit(solution)/shard_map/densities/pallas_call | solution.py:848
  60.3 2.8 %copy.6 = f32[256,1,768]{2,1,0:T(1,128)} copy(f32[256,1,768]{2,0,1:T(8,128)} %bitcast.2) | data formatting | bytes 1572864
  63.1 1.5 %copy.8 = f32[24,768]{1,0:T(8,128)} copy(f32[24,768]{1,0:T(8,128)} %get-tuple-element.11) | data formatting | bytes 147456

commit v3 on v2

--- a/solution.py
+++ b/solution.py
@@ -413,10 +413,10 @@
 def paired_kernel(
     n, occ_e, half, coef, vir_e, three_out, vir_out,
     ints, raw, full, own, held, gift, cross, amps, vir,
-    t_give, t_got, n_give, n_got, v_pair, v_line, v_col, v_far,
+    t_give, t_got, n_give, n_got, near_sum, v_pair, v_line, v_col,
     t_code, t_scale, t_code_in, t_scale_in, x_code, x_scale, x_code_in, x_scale_in,
-    z_code, z_scale, z_code_in, z_scale_in,
-    i_sem, keep_sem, o_sem, raw_sems, c_recv, c_up, c_down, c_side, cp_send, cp_recv,
+    z_code, z_scale, z_code_in, z_scale_in, y_code, y_scale, y_code_in, y_scale_in, energies, levels,
+    e_sems, i_sem, keep_sem, o_sem, raw_sems, c_recv, c_up, c_down, c_side, c_jump, cp_send, cp_recv,
     pn_sems, pf_sems, f_recv, f_send, z_fwd, x_fwd, y_send, g_send, g_recv,
     t_sems, ts_send, ts_recv, n_sems, vp_send, vp_recv, x_send, x_recv, z_send, z_recv, yv_send, yv_recv,
 ):
@@ -454,10 +454,13 @@
     peers += [(2 * ((z + d) % nz) + low, t) for d in range(1, nz) for t in (s, other)]
     for peer in peers:
         pl.semaphore_signal(barrier, inc=1, device_id=peer, device_id_type=MESH)
+    small = [pltpu.make_async_copy(occ_e, energies, e_sems.at[0]), pltpu.make_async_copy(vir_e, levels, e_sems.at[1])]
     fetch = pltpu.make_async_copy(half, ints, i_sem)
     fetch.start()
     keep = pltpu.make_async_copy(coef, full.at[span(o, part)], keep_sem)
     keep.start()
+    for copy in small:
+        copy.start()
     pl.semaphore_wait(barrier, len(peers))
 
     lend = remote(half.at[o], raw, raw_sems.at[0], raw_sems.at[1], opposite)
@@ -470,10 +473,10 @@
         block = 2 * chain + low
         dst = coef_slot(block, c, h)
         recv = c_recv.at[block, h]
-        pl.when(jnp.logical_and(chain <= z, z < nz - 1))(
+        pl.when(jnp.logical_and(jnp.logical_and(chain <= z, chain > z - 2), z < nz - 1))(
             lambda: act(remote(src, dst, c_up.at[chain, h], recv, (above, s)))
         )
-        pl.when(jnp.logical_and(chain >= z, z > 0))(
+        pl.when(jnp.logical_and(jnp.logical_and(chain >= z, chain < z + 2), z > 0))(
             lambda: act(remote(src, dst, c_down.at[chain, h], recv, (below, s)))
         )
         act(remote(src, dst, c_side.at[chain, h], recv, (side, s)))
@@ -486,9 +489,23 @@
         ref = coef_slot(block, c, h)
         remote(ref, ref, c_side.at[0, h], c_recv.at[block, h], (side, s)).wait_recv()
 
+    def coef_far(h, act):
+        src = coef.at[:, pl.ds(pl.multiple_of((pieces * c + h) * piece, piece), piece)]
+        recv = c_recv.at[o, h]
+        for d in range(3, nz):
+            pl.when(z + d < nz)(
+                lambda: act(remote(src, coef_slot(o, c, h), c_jump.at[0, d, h], recv, (o + 2 * d, s)))
+            )
+            pl.when(z >= d)(
+                lambda: act(remote(src, coef_slot(o, c, h), c_jump.at[1, d, h], recv, (o - 2 * d, s)))
+            )
+
     for h in range(pieces):
+        coef_far(h, start)
         coef_relay(z, h, coef.at[:, pl.ds(pl.multiple_of((pieces * c + h) * piece, piece), piece)], start)
-    row_e = vir_e[...].reshape(1, virtuals)
+    for copy in small:
+        copy.wait()
+    row_e = levels[...].reshape(1, virtuals)
     here = lax.broadcasted_iota(jnp.int32, (width, virtuals), 0) + s * width
     there = lax.broadcasted_iota(jnp.int32, (width, virtuals), 1)
     col_e = jnp.sum(jnp.where(here == there, row_e, 0.0), axis=1, keepdims=True)
@@ -637,7 +654,7 @@
         coulomb = lax.dot_general(
             held[rows, :], own[...], (((1,), (1,)), ((), ())), preferred_element_type=F32
         )
-        left = jnp.concatenate([occ_e[o] + occ_e[2 * chain + t] - col_e for t in range(2)], axis=0)
+        left = jnp.concatenate([energies[o] + energies[2 * chain + t] - col_e for t in range(2)], axis=0)
         amps[rows, :] = (coulomb / (left - row_e)).astype(jnp.bfloat16)
 
     @pl.loop(0, nz)
@@ -716,7 +733,7 @@
         return remote(vir.at[chain, :, :, 1 - c], v_pair.at[chain], vp_send.at[chain], vp_recv.at[chain], partner)
 
     def between():
-        return remote(v_col.at[far], v_far, yv_send, yv_recv, opposite)
+        return coded_copies(y_code, y_scale, y_code_in, y_scale_in, (yv_send, yv_recv), opposite)
 
     near_swap = remote(n_give, n_got, n_sems.at[0], n_sems.at[1], partner)
     first = jnp.where(z < nz // 2, 1, 0)
@@ -749,29 +766,44 @@
         far_swap(k).wait_recv()
         encode(new + t_got[k], t_code.at[k], t_scale.at[k])
         both_start(far_send(k))
-    n_give[...] = part_three(q, 1 - c, slice(None))
-    near_swap.start()
-    three_out[...] = part_three(q, c, slice(None))
-    for chain in farthest:
+    def add_beside(chain, last):
         both_recv(x_swap(chain))
         total = pair_sum(chain, low) + decode(x_code_in.at[chain], x_scale_in.at[chain])
-        v_line[...] = total
-        if chain is not farthest[-1]:
+        if last:
+            v_line[...] = total
+        else:
             encode(total, z_code.at[chain], z_scale.at[chain])
             both_start(along(chain, z))
+
+    def near_give():
+        n_give[...] = part_three(q, 1 - c, slice(None))
+        near_swap.start()
+
+    def near_keep():
+        near_sum[...] = part_three(q, c, slice(None))
+
+    fillers = [near_give, near_keep]
+    for k in range(nz):
+        add_beside(farthest[k], k == nz - 1)
+        if k < len(fillers):
+            fillers[k]()
+    for filler in fillers[nz:]:
+        filler()
     near_swap.wait_recv()
-    three_out[...] += n_got[...]
+    near_sum[...] += n_got[...]
     for k in range(1, nz):
         sender = nearest(k)
         both_recv(along(sender, sender))
         v_line[...] += decode(z_code_in.at[sender], z_scale_in.at[sender])
     v_col[...] = v_line[...].reshape(v_col.shape)
-    between().start()
+    encode(v_col[far], y_code, y_scale)
+    both_start(between())
     for k in range(strips):
         both_recv(far_send(k))
-        three_out[:, wide(k)] += decode(t_code_in.at[k], t_scale_in.at[k])
-    between().wait_recv()
-    vir_out[...] = (v_col[q] + v_far[...]) / (n * virtuals)
+        near_sum[:, wide(k)] += decode(t_code_in.at[k], t_scale_in.at[k])
+    three_out[...] = near_sum[...].reshape(three_out.shape)
+    both_recv(between())
+    vir_out[...] = (v_col[q] + decode(y_code_in, y_scale_in)) / (n * virtuals)
 
     lend.wait_send()
 
@@ -779,6 +811,9 @@
     def _(chain):
         for h in range(pieces):
             coef_relay(chain, h, coef_slot(2 * chain + low, c, h), sent)
+
+    for h in range(pieces):
+        coef_far(h, sent)
 
     @pl.loop(1, n)
     def _(d):
@@ -804,7 +839,7 @@
         both_sent(x_swap(chain))
     for k in range(1, nz):
         both_sent(along(nearest(k), z))
-    between().wait_send()
+    both_sent(between())
 
 
 def paired(n, half_integrals, coef, occ_energy, vir_energy):
@@ -831,26 +866,29 @@
         packed(n * width, 4 * tile), packed(n, width, tile), packed(n, 2 * width, tile), packed(n * width, virtuals),
         room(nz, 2, 2, 2, rows, virtuals),
         room(strips, tile, strip), room(strips, tile, strip), room(tile, virtuals), room(tile, virtuals),
-        room(nz, 2, 2, rows, virtuals), room(2 * rows, virtuals), room(2, rows, virtuals), room(rows, virtuals),
+        room(tile, virtuals), room(nz, 2, 2, rows, virtuals), room(2 * rows, virtuals), room(2, rows, virtuals),
     ]
     groups = tile // 32
     for _ in range(2):
         scratch += [packed(strips, tile, strip), room(strips, groups, 1, strip)]
     for _ in range(4):
         scratch += [packed(nz, 2 * rows, virtuals), room(nz, 2, 1, virtuals)]
+    for _ in range(2):
+        scratch += [packed(rows, virtuals), room(1, 1, virtuals)]
+    scratch += [pltpu.SMEM((n,), F32), room(virtuals)]
     scratch += [
-        dma, dma, dma, dma((2,)), dma((n, pieces)), dma((nz, pieces)), dma((nz, pieces)), dma((nz, pieces)),
+        dma((2,)), dma, dma, dma, dma((2,)), dma((n, pieces)), dma((nz, pieces)), dma((nz, pieces)), dma((nz, pieces)), dma((2, nz, pieces)),
         dma((n, pieces)), dma((n, pieces)),
         dma((2,)), dma((2,)), dma((n, 2)), dma((3, 2)), dma((2, 2)), dma((2,)), dma((n, 2)), dma((n,)), dma((n,)),
         dma((2, strips)), dma((strips, 2)), dma((strips, 2)), dma((2,)),
-        dma((nz,)), dma((nz,)), dma((nz, 2)), dma((nz, 2)), dma((nz, 2)), dma((nz, 2)), dma, dma,
+        dma((nz,)), dma((nz,)), dma((nz, 2)), dma((nz, 2)), dma((nz, 2)), dma((nz, 2)), dma((2,)), dma((2,)),
     ]
     return pl.pallas_call(
         functools.partial(paired_kernel, n),
         out_shape=(
-            jax.ShapeDtypeStruct((tile, virtuals), F32), jax.ShapeDtypeStruct((rows, virtuals), F32),
+            pltpu.VMEM((tile, 1, virtuals), F32), pltpu.VMEM((rows, virtuals), F32),
         ),
-        in_specs=[pl.BlockSpec(memory_space=pltpu.SMEM), pl.BlockSpec(memory_space=pl.ANY), vmem, vmem],
+        in_specs=[pl.BlockSpec(memory_space=pl.ANY)] * 4,
         out_specs=(vmem, vmem),
         scratch_shapes=scratch,
         compiler_params=pltpu.CompilerParams(
@@ -868,7 +906,7 @@
     virtuals = part * n
     if nq == 2 and n % 2 == 0 and nz > 1 and nz % 2 == 0 and virtuals % (32 * n) == 0 and virtuals % 256 == 0 and tile % 32 == 0:
         three, vir_rows = paired(n, half_integrals, vir_coef.T, occ_energy, vir_energy)
-        return three[:, None, :], vir_rows
+        return three, vir_rows
     width, rows = virtuals // aux, virtuals // (n * aux)
     vmem = pl.BlockSpec(memory_space=pltpu.VMEM)
     dma = pltpu.SemaphoreType.DMA

time: 64.8 us -> 58.6 us (0.904)
  Pallas kernels: 59.6 us -> 56.3 us
  local copies, waits for them, and re-layouts: 4.34 us -> 1.51 us
    pallas_call x1, Pallas kernels: 59.6 us -> 56.3 us  [paired(): pl.pallas_call(functools.partial(paired_kernel, n), out_shape=(pltpu.VMEM...]
    unnamed x2, local copies, waits for them, and re-layouts: 4.34 us -> 1.51 us
where the time goes in v3:
time: 58.6 us; the launch traced here: 58.4 us
  Pallas kernels  56.3 us (96%)
  local copies, waits for them, and re-layouts  1.51 us (3%)
  between operations  0.64 us (1%)
    pallas_call x1, Pallas kernels, paired(): pl.pallas_call(functools.partial(paired_kernel, n), out_shape=(pltpu.VMEM...  56.3 us
    unnamed x2, local copies, waits for them, and re-layouts  1.51 us

profile of v3, /device:TPU:0, one launch (start us, length us, event | category | flops | bytes accessed | tf_op | source)
XLA Modules:
  0.0 58.4 jit_solution(5469152935028525409)
XLA Ops:
  0.6 56.3 %densities.1 = (f32[256,1,768]{2,1,0:T(1,128)S(1)}, f32[24,768]{1,0:T(8,128)S(1)}) custom-call(f32[8]{0:T(128)} %occ_e.1, bf16[8,256,1024]{2,1,0:T(8,128)(2,1)} %half.1, bf16[96,1024]{1,0:T(8,128)(2,1)} %bitcast.1, f32[768]{0:T(1024)} %vir_e.1), custom_call_target="tpu_custom_call" | custom-call | tf_op jit(solution)/shard_map/densities/pallas_call | solution.py:886
  56.9 0.9 %copy.8 = f32[256,1,768]{2,1,0:T(1,128)} copy(f32[256,1,768]{2,1,0:T(1,128)S(1)} %get-tuple-element.2) | data formatting | bytes 1572864
  57.8 0.6 %copy.9 = f32[24,768]{1,0:T(8,128)} copy(f32[24,768]{1,0:T(8,128)S(1)} %get-tuple-element.3) | data formatting | bytes 147456

commit v4 on v3

--- a/solution.py
+++ b/solution.py
@@ -416,9 +416,9 @@
     t_give, t_got, n_give, n_got, near_sum, v_pair, v_line, v_col,
     t_code, t_scale, t_code_in, t_scale_in, x_code, x_scale, x_code_in, x_scale_in,
     z_code, z_scale, z_code_in, z_scale_in, y_code, y_scale, y_code_in, y_scale_in, energies, levels,
-    e_sems, i_sem, keep_sem, o_sem, raw_sems, c_recv, c_up, c_down, c_side, c_jump, cp_send, cp_recv,
-    pn_sems, pf_sems, f_recv, f_send, z_fwd, x_fwd, y_send, g_send, g_recv,
-    t_sems, ts_send, ts_recv, n_sems, vp_send, vp_recv, x_send, x_recv, z_send, z_recv, yv_send, yv_recv,
+    e_sems, i_sem, keep_sem, o_sem, raw_sems, c_recv, c_up, c_down, c_side, c_jump, cp_sems,
+    pn_sems, pf_sems, f_recv, f_send, z_fwd, x_fwd, y_send, g_sems,
+    t_send, t_recv, ts_send, ts_recv, n_sems, vp_send, vp_recv, x_send, x_recv, z_send, z_recv, yv_send, yv_recv,
 ):
     o = lax.axis_index("occ")
     s = lax.axis_index("aux")
@@ -469,40 +469,38 @@
     def coef_slot(block, core, h):
         return full.at[span(block, part), pl.ds(pl.multiple_of((pieces * core + h) * piece, piece), piece)]
 
-    def coef_relay(chain, h, src, act):
-        block = 2 * chain + low
-        dst = coef_slot(block, c, h)
-        recv = c_recv.at[block, h]
+    def coef_relay(chain, src, dst, recv, act):
         pl.when(jnp.logical_and(jnp.logical_and(chain <= z, chain > z - 2), z < nz - 1))(
-            lambda: act(remote(src, dst, c_up.at[chain, h], recv, (above, s)))
+            lambda: act(remote(src, dst, c_up.at[z - chain], recv, (above, s)))
         )
         pl.when(jnp.logical_and(jnp.logical_and(chain >= z, chain < z + 2), z > 0))(
-            lambda: act(remote(src, dst, c_down.at[chain, h], recv, (below, s)))
-        )
-        act(remote(src, dst, c_side.at[chain, h], recv, (side, s)))
+            lambda: act(remote(src, dst, c_down.at[chain - z], recv, (below, s)))
+        )
+        act(remote(src, dst, c_side.at[chain], recv, (side, s)))
 
     def coef_across(block, h, core):
         ref = coef_slot(block, core, h)
-        return remote(ref, ref, cp_send.at[block, h], cp_recv.at[block, h], partner)
+        return remote(ref, ref, cp_sems.at[0], cp_sems.at[1], partner)
 
     def coef_wait(block, h):
         ref = coef_slot(block, c, h)
-        remote(ref, ref, c_side.at[0, h], c_recv.at[block, h], (side, s)).wait_recv()
-
-    def coef_far(h, act):
-        src = coef.at[:, pl.ds(pl.multiple_of((pieces * c + h) * piece, piece), piece)]
-        recv = c_recv.at[o, h]
+        remote(ref, ref, c_side.at[0], c_recv.at[block, h], (side, s)).wait_recv()
+
+    def coef_own(h):
+        return coef.at[:, pl.ds(pl.multiple_of((pieces * c + h) * piece, piece), piece)]
+
+    def coef_far(src, dst, recv, act):
         for d in range(3, nz):
             pl.when(z + d < nz)(
-                lambda: act(remote(src, coef_slot(o, c, h), c_jump.at[0, d, h], recv, (o + 2 * d, s)))
+                lambda: act(remote(src, dst, c_jump.at[0, d], recv, (o + 2 * d, s)))
             )
             pl.when(z >= d)(
-                lambda: act(remote(src, coef_slot(o, c, h), c_jump.at[1, d, h], recv, (o - 2 * d, s)))
+                lambda: act(remote(src, dst, c_jump.at[1, d], recv, (o - 2 * d, s)))
             )
 
     for h in range(pieces):
-        coef_far(h, start)
-        coef_relay(z, h, coef.at[:, pl.ds(pl.multiple_of((pieces * c + h) * piece, piece), piece)], start)
+        coef_far(coef_own(h), coef_slot(o, c, h), c_recv.at[o, h], start)
+        coef_relay(z, coef_own(h), coef_slot(o, c, h), c_recv.at[o, h], start)
     for copy in small:
         copy.wait()
     row_e = levels[...].reshape(1, virtuals)
@@ -522,17 +520,17 @@
         block = 2 * chain + low
         for h in range(pieces):
             coef_wait(block, h)
-            coef_relay(chain, h, coef_slot(block, c, h), start)
+            coef_relay(chain, coef_slot(block, c, h), coef_slot(block, c, h), c_recv.at[block, h], start)
             coef_across(block, h, c).start()
         coef_beside(k - 1)
 
     coef_beside(nz - 1)
 
-    @pl.loop(1, n)
-    def _(d):
-        block = (o + d) % n
-        for h in range(pieces):
-            coef_across(block, h, 1 - c).wait_recv()
+    def coef_halves(blocks):
+        ref = full.at[: blocks * part, : basis // 2]
+        return remote(ref, ref, cp_sems.at[0], cp_sems.at[1], partner)
+
+    coef_halves(n - 1).wait_recv()
 
     keep.wait()
     fetch.wait()
@@ -543,30 +541,27 @@
     def cols(group, core):
         return span(2 * group + core, tile)
 
-    def lend_block(block, act):
+    def lend_block(block, sem, act):
         for core in range(2):
             act(
                 remote(
                     cross.at[block, pl.ds(core * width, width)], held.at[span(block, width), cols(q, c)],
-                    y_send.at[block, core], f_recv.at[block, c], (o, 2 * far + core),
+                    y_send.at[sem], f_recv.at[block], (o, 2 * far + core),
                 )
             )
 
     def distant(chain):
         return jnp.abs(chain - z) > 2
 
-    def lend_blocks(k, act):
-        chain = nearest(k)
-        act(2 * chain + 1 - low)
-        pl.when(distant(chain))(lambda: act(2 * chain + low))
-
-    def cross_over(block):
+    def cross_over(block, sem):
         cross[block] = transform(full[span(far, 2 * width), :], ints[block])
-        lend_block(block, start)
+        lend_block(block, sem, start)
 
     @pl.loop(2, nz)
     def _(k):
-        lend_blocks(k, cross_over)
+        chain = nearest(k)
+        cross_over(2 * chain + 1 - low, 0)
+        pl.when(distant(chain))(lambda: cross_over(2 * chain + low, k - 1))
 
     def own_part(group, core):
         return own.at[:, cols(group, core)]
@@ -579,28 +574,29 @@
         ref = own_part(far, core)
         return remote(ref, ref, pf_sems.at[0], pf_sems.at[1], partner)
 
-    def hand_out(act):
-        for core in range(2):
-            src = own.at[span(2 * q + core, width), cols(far, c)]
-            dst = held.at[span(o, width), cols(far, c)]
-            recv = f_recv.at[o, c]
-            pl.when(z < nz - 1)(lambda: act(remote(src, dst, f_send.at[0, core], recv, (above, 2 * q + core))))
-            pl.when(z > 0)(lambda: act(remote(src, dst, f_send.at[1, core], recv, (below, 2 * q + core))))
-        for core in range(2):
-            src = own.at[span(2 * q + core, width), cols(far, c)]
-            dst = held.at[span(o, width), cols(far, c)]
-            act(remote(src, dst, f_send.at[2, core], f_recv.at[o, c], (side, 2 * q + core)))
+    def hand_out(pairs, act):
+        for core, src, dst in pairs:
+            recv = f_recv.at[o]
+            pl.when(z < nz - 1)(lambda: act(remote(src, dst, f_send.at[0], recv, (above, 2 * q + core))))
+            pl.when(z > 0)(lambda: act(remote(src, dst, f_send.at[1], recv, (below, 2 * q + core))))
+        for core, src, dst in pairs:
+            act(remote(src, dst, f_send.at[2], f_recv.at[o], (side, 2 * q + core)))
+
+    outgoing = [
+        (core, own.at[span(2 * q + core, width), cols(far, c)], held.at[span(o, width), cols(far, c)])
+        for core in range(2)
+    ]
 
     lend.wait_recv()
     own[:, cols(far, c)] = transform(full[...], raw[...])
-    hand_out(start)
+    hand_out(outgoing, start)
     far_part(c).start()
     own[:, cols(q, c)] = transform(full[...], ints[o])
     near_part(c).start()
 
     def give(block, core):
         return remote(
-            gift.at[block], held.at[span(block, width), cols(q, core)], g_send.at[block], g_recv.at[block], partner
+            gift.at[block], held.at[span(block, width), cols(q, core)], g_sems.at[0], g_sems.at[1], partner
         )
 
     @pl.loop(1, n)
@@ -612,31 +608,26 @@
         gift[block] = both[width:]
         give(block, c).start()
 
+    def given():
+        ref = gift.at[: n - 1]
+        return remote(ref, ref, g_sems.at[0], g_sems.at[1], partner)
+
     far_part(1 - c).wait_recv()
     near_part(1 - c).wait_recv()
     mine = pltpu.make_async_copy(own.at[span(s, width)], held.at[span(o, width)], o_sem)
     mine.start()
 
-    def far_slot(block, core):
-        return held.at[span(block, width), cols(far, core)]
-
     def arrive(block):
-        for core in range(2):
-            ref = far_slot(block, core)
-            remote(ref, ref, x_fwd.at[0], f_recv.at[block, core], (side, s)).wait_recv()
+        ref = held.at[span(block, width), span(far, 2 * tile)]
+        remote(ref, ref, x_fwd, f_recv.at[block], (side, s)).wait_recv()
 
     def pass_on(chain, act):
         block = 2 * chain + low
-        for core in range(2):
-            ref = far_slot(block, core)
-            recv = f_recv.at[block, core]
-            pl.when(jnp.logical_and(chain < z, z < nz - 1))(
-                lambda: act(remote(ref, ref, z_fwd.at[0, core], recv, (above, s)))
-            )
-            pl.when(jnp.logical_and(chain > z, z > 0))(
-                lambda: act(remote(ref, ref, z_fwd.at[1, core], recv, (below, s)))
-            )
-            pl.when(chain == nearest(1))(lambda: act(remote(ref, ref, x_fwd.at[core], recv, (side, s))))
+        ref = held.at[span(block, width), span(far, 2 * tile)]
+        recv = f_recv.at[block]
+        pl.when(jnp.logical_and(chain < z, z < nz - 1))(lambda: act(remote(ref, ref, z_fwd.at[0], recv, (above, s))))
+        pl.when(jnp.logical_and(chain > z, z > 0))(lambda: act(remote(ref, ref, z_fwd.at[1], recv, (below, s))))
+        pl.when(chain == nearest(1))(lambda: act(remote(ref, ref, x_fwd, recv, (side, s))))
 
     def beside_each(act):
         pl.when(z > 0)(lambda: act(z - 1))
@@ -647,6 +638,7 @@
         pass_on(chain, start)
 
     beside_each(take)
+    given().wait_recv()
     mine.wait()
 
     def absorb(chain):
@@ -662,8 +654,6 @@
         chain = nearest(jnp.where(i == 0, 0, jnp.where(i == nz - 1, 1, i + 1)))
         pl.when(jnp.abs(chain - z) > 1)(lambda: arrive(2 * chain + low))
         arrive(2 * chain + 1 - low)
-        pl.when(chain != z)(lambda: give(2 * chain + low, 1 - c).wait_recv())
-        give(2 * chain + 1 - low, 1 - c).wait_recv()
         absorb(chain)
 
     contract = (((0,), (0,)), ((), ()))
@@ -680,7 +670,7 @@
         )
 
     def far_swap(k):
-        return remote(t_give.at[k], t_got.at[k], t_sems.at[0, k], t_sems.at[1, k], partner)
+        return remote(t_give.at[k], t_got.at[k], t_send, t_recv.at[k], partner)
 
     def coded_copies(code, scale, code_to, scale_to, sems, target):
         return (
@@ -689,17 +679,17 @@
         )
 
     def far_send(k):
-        sems = (ts_send.at[k], ts_recv.at[k])
+        sems = (ts_send, ts_recv.at[k])
         return coded_copies(t_code.at[k], t_scale.at[k], t_code_in.at[k], t_scale_in.at[k], sems, opposite)
 
     def x_swap(chain):
-        sems = (x_send.at[chain], x_recv.at[chain])
+        sems = (x_send, x_recv.at[chain])
         return coded_copies(
             x_code.at[chain], x_scale.at[chain], x_code_in.at[chain], x_scale_in.at[chain], sems, (side, s)
         )
 
     def along(to, sender):
-        sems = (z_send.at[to], z_recv.at[sender])
+        sems = (z_send, z_recv.at[sender])
         return coded_copies(
             z_code.at[to], z_scale.at[to], z_code_in.at[sender], z_scale_in.at[sender], sems, (2 * to + low, s)
         )
@@ -730,7 +720,7 @@
         return (words * (scale[...] * (1.0 / SPAN))).reshape(code.shape)
 
     def v_swap(chain):
-        return remote(vir.at[chain, :, :, 1 - c], v_pair.at[chain], vp_send.at[chain], vp_recv.at[chain], partner)
+        return remote(vir.at[chain, :, :, 1 - c], v_pair.at[chain], vp_send, vp_recv.at[chain], partner)
 
     def between():
         return coded_copies(y_code, y_scale, y_code_in, y_scale_in, (yv_send, yv_recv), opposite)
@@ -807,38 +797,38 @@
 
     lend.wait_send()
 
+    half_block = full.at[:part, : basis // 2]
+
     @pl.loop(0, nz)
     def _(chain):
-        for h in range(pieces):
-            coef_relay(chain, h, coef_slot(2 * chain + low, c, h), sent)
-
-    for h in range(pieces):
-        coef_far(h, sent)
-
-    @pl.loop(1, n)
-    def _(d):
-        block = (o + d) % n
-        for h in range(pieces):
-            coef_across(block, h, c).wait_send()
-        give(block, c).wait_send()
-
-    @pl.loop(2, nz)
-    def _(k):
-        lend_blocks(k, lambda block: lend_block(block, sent))
-
-    hand_out(sent)
+        coef_relay(chain, half_block, half_block, c_recv.at[0, 0], sent)
+
+    coef_far(half_block, half_block, c_recv.at[0, 0], sent)
+    coef_halves(n - 1).wait_send()
+    given().wait_send()
+
+    def lent(blocks, sem):
+        ref = cross.at[:blocks]
+        return remote(ref, ref, y_send.at[sem], f_recv.at[0], opposite)
+
+    if nz > 2:
+        lent(nz - 2, 0).wait_send()
+    for k in range(2, nz):
+        pl.when(distant(nearest(k)))(lambda: lent(1, k - 1).wait_send())
+
+    both_rows = own.at[: 2 * width, :tile]
+    hand_out([(0, both_rows, both_rows)], sent)
     far_part(c).wait_send()
     near_part(c).wait_send()
     beside_each(lambda chain: pass_on(chain, sent))
     near_swap.wait_send()
-    for k in range(strips):
-        far_swap(k).wait_send()
-        both_sent(far_send(k))
-    for chain in range(nz):
-        v_swap(chain).wait_send()
-        both_sent(x_swap(chain))
-    for k in range(1, nz):
-        both_sent(along(nearest(k), z))
+    remote(t_give, t_give, t_send, t_recv.at[0], partner).wait_send()
+    both_sent(coded_copies(t_code, t_scale, t_code, t_scale, (ts_send, ts_recv.at[0]), opposite))
+    whole = vir.at[:, :, :, 0]
+    remote(whole, whole, vp_send, vp_recv.at[0], partner).wait_send()
+    both_sent(coded_copies(x_code, x_scale, x_code, x_scale, (x_send, x_recv.at[0]), (side, s)))
+    codes, scales = z_code.at[: nz - 1], z_scale.at[: nz - 1]
+    both_sent(coded_copies(codes, scales, codes, scales, (z_send, z_recv.at[0]), (side, s)))
     both_sent(between())
 
 
@@ -877,11 +867,10 @@
         scratch += [packed(rows, virtuals), room(1, 1, virtuals)]
     scratch += [pltpu.SMEM((n,), F32), room(virtuals)]
     scratch += [
-        dma((2,)), dma, dma, dma, dma((2,)), dma((n, pieces)), dma((nz, pieces)), dma((nz, pieces)), dma((nz, pieces)), dma((2, nz, pieces)),
-        dma((n, pieces)), dma((n, pieces)),
-        dma((2,)), dma((2,)), dma((n, 2)), dma((3, 2)), dma((2, 2)), dma((2,)), dma((n, 2)), dma((n,)), dma((n,)),
-        dma((2, strips)), dma((strips, 2)), dma((strips, 2)), dma((2,)),
-        dma((nz,)), dma((nz,)), dma((nz, 2)), dma((nz, 2)), dma((nz, 2)), dma((nz, 2)), dma((2,)), dma((2,)),
+        dma((2,)), dma, dma, dma, dma((2,)), dma((n, pieces)), dma((2,)), dma((2,)), dma((nz,)), dma((2, nz)), dma((2,)),
+        dma((2,)), dma((2,)), dma((n,)), dma((3,)), dma((2,)), dma, dma((nz,)), dma((2,)),
+        dma, dma((strips,)), dma((2,)), dma((strips, 2)), dma((2,)), dma, dma((nz,)),
+        dma((2,)), dma((nz, 2)), dma((2,)), dma((nz, 2)), dma((2,)), dma((2,)),
     ]
     return pl.pallas_call(
         functools.partial(paired_kernel, n),

time: 58.6 us -> 56.5 us (0.964)
  Pallas kernels: 56.3 us -> 54.2 us
    pallas_call x1, Pallas kernels: 56.3 us -> 54.2 us  [paired(): pl.pallas_call(functools.partial(paired_kernel, n), out_shape=(pltpu.VMEM...]
where the time goes in v4:
time: 56.5 us; the launch traced here: 56.4 us
  Pallas kernels  54.2 us (96%)
  local copies, waits for them, and re-layouts  1.51 us (3%)
  between operations  0.64 us (1%)
    pallas_call x1, Pallas kernels, paired(): pl.pallas_call(functools.partial(paired_kernel, n), out_shape=(pltpu.VMEM...  54.2 us
    unnamed x2, local copies, waits for them, and re-layouts  1.51 us

profile of v4, /device:TPU:0, one launch (start us, length us, event | category | flops | bytes accessed | tf_op | source)
XLA Modules:
  0.0 56.4 jit_solution(15772022858798525043)
XLA Ops:
  0.6 54.2 %densities.1 = (f32[256,1,768]{2,1,0:T(1,128)S(1)}, f32[24,768]{1,0:T(8,128)S(1)}) custom-call(f32[8]{0:T(128)} %occ_e.1, bf16[8,256,1024]{2,1,0:T(8,128)(2,1)} %half.1, bf16[96,1024]{1,0:T(8,128)(2,1)} %bitcast.1, f32[768]{0:T(1024)} %vir_e.1), custom_call_target="tpu_custom_call" | custom-call | tf_op jit(solution)/shard_map/densities/pallas_call | solution.py:875
  54.9 0.9 %copy.8 = f32[256,1,768]{2,1,0:T(1,128)} copy(f32[256,1,768]{2,1,0:T(1,128)S(1)} %get-tuple-element.2) | data formatting | bytes 1572864
  55.8 0.6 %copy.9 = f32[24,768]{1,0:T(8,128)} copy(f32[24,768]{1,0:T(8,128)S(1)} %get-tuple-element.3) | data formatting | bytes 147456

commit v5 on v4

--- a/solution.py
+++ b/solution.py
@@ -413,7 +413,7 @@
 def paired_kernel(
     n, occ_e, half, coef, vir_e, three_out, vir_out,
     ints, raw, full, own, held, gift, cross, amps, vir,
-    t_give, t_got, n_give, n_got, near_sum, v_pair, v_line, v_col,
+    t_give, t_mine, t_got, n_give, n_got, near_sum, v_pair, v_line, v_col,
     t_code, t_scale, t_code_in, t_scale_in, x_code, x_scale, x_code_in, x_scale_in,
     z_code, z_scale, z_code_in, z_scale_in, y_code, y_scale, y_code_in, y_scale_in, energies, levels,
     e_sems, i_sem, keep_sem, o_sem, raw_sems, c_recv, c_up, c_down, c_side, c_jump, cp_sems,
@@ -449,6 +449,11 @@
     def nearest(k):
         return nearest_first(z, k, nz)
 
+    at_end = jnp.logical_or(z == 0, z == nz - 1)
+    inner_order = [0] + list(range(2, nz)) + [1]
+    end_order = [0, nz - 1] + list(range(1, nz - 1))
+    order = [nearest(jnp.where(at_end, a, b)) for a, b in zip(end_order, inner_order)]
+
     barrier = pltpu.get_barrier_semaphore()
     peers = [partner, opposite, (o, 2 * far + 1 - c), (side, s), (side, other)]
     peers += [(2 * ((z + d) % nz) + low, t) for d in range(1, nz) for t in (s, other)]
@@ -499,8 +504,9 @@
             )
 
     for h in range(pieces):
+        coef_relay(z, coef_own(h), coef_slot(o, c, h), c_recv.at[o, h], start)
+    for h in range(pieces):
         coef_far(coef_own(h), coef_slot(o, c, h), c_recv.at[o, h], start)
-        coef_relay(z, coef_own(h), coef_slot(o, c, h), c_recv.at[o, h], start)
     for copy in small:
         copy.wait()
     row_e = levels[...].reshape(1, virtuals)
@@ -508,23 +514,31 @@
     there = lax.broadcasted_iota(jnp.int32, (width, virtuals), 1)
     col_e = jnp.sum(jnp.where(here == there, row_e, 0.0), axis=1, keepdims=True)
 
-    def coef_beside(k):
-        block = 2 * nearest(k) + 1 - low
+    def each_at(d, act):
+        pl.when(z + d < nz)(lambda: act(z + d))
+        pl.when(z >= d)(lambda: act(z - d))
+
+    def coef_beside(chain, h):
+        block = 2 * chain + 1 - low
+        coef_wait(block, h)
+        coef_across(block, h, c).start()
+
+    def coef_along(chain, h):
+        block = 2 * chain + low
+        slot = coef_slot(block, c, h)
+        coef_wait(block, h)
+        coef_relay(chain, slot, slot, c_recv.at[block, h], start)
+        coef_across(block, h, c).start()
+
+    for d in range(1, nz + 1):
         for h in range(pieces):
-            coef_wait(block, h)
-            coef_across(block, h, c).start()
-
-    @pl.loop(1, nz)
-    def _(k):
-        chain = nearest(k)
-        block = 2 * chain + low
+            if d < nz:
+                each_at(d, lambda chain: coef_along(chain, h))
         for h in range(pieces):
-            coef_wait(block, h)
-            coef_relay(chain, coef_slot(block, c, h), coef_slot(block, c, h), c_recv.at[block, h], start)
-            coef_across(block, h, c).start()
-        coef_beside(k - 1)
-
-    coef_beside(nz - 1)
+            if d == 1:
+                coef_beside(z, h)
+            else:
+                each_at(d - 1, lambda chain: coef_beside(chain, h))
 
     def coef_halves(blocks):
         ref = full.at[: blocks * part, : basis // 2]
@@ -546,7 +560,7 @@
             act(
                 remote(
                     cross.at[block, pl.ds(core * width, width)], held.at[span(block, width), cols(q, c)],
-                    y_send.at[sem], f_recv.at[block], (o, 2 * far + core),
+                    y_send.at[sem], f_recv.at[block, 0], (o, 2 * far + core),
                 )
             )
 
@@ -559,9 +573,9 @@
 
     @pl.loop(2, nz)
     def _(k):
-        chain = nearest(k)
+        chain = nearest(jnp.where(at_end, nz + 1 - k, k))
         cross_over(2 * chain + 1 - low, 0)
-        pl.when(distant(chain))(lambda: cross_over(2 * chain + low, k - 1))
+        pl.when(distant(chain))(lambda: cross_over(2 * chain + low, jnp.where(at_end, nz - k, k - 1)))
 
     def own_part(group, core):
         return own.at[:, cols(group, core)]
@@ -574,22 +588,23 @@
         ref = own_part(far, core)
         return remote(ref, ref, pf_sems.at[0], pf_sems.at[1], partner)
 
-    def hand_out(pairs, act):
-        for core, src, dst in pairs:
-            recv = f_recv.at[o]
-            pl.when(z < nz - 1)(lambda: act(remote(src, dst, f_send.at[0], recv, (above, 2 * q + core))))
-            pl.when(z > 0)(lambda: act(remote(src, dst, f_send.at[1], recv, (below, 2 * q + core))))
-        for core, src, dst in pairs:
-            act(remote(src, dst, f_send.at[2], f_recv.at[o], (side, 2 * q + core)))
-
-    outgoing = [
-        (core, own.at[span(2 * q + core, width), cols(far, c)], held.at[span(o, width), cols(far, c)])
-        for core in range(2)
-    ]
+    def hand_out(parts, act):
+        for core, t, src, dst in parts:
+            recv = f_recv.at[o, t]
+            to = 2 * q + core
+            pl.when(z < nz - 1)(lambda: act(remote(src, dst, f_send.at[0], recv, (above, to))))
+            pl.when(z > 0)(lambda: act(remote(src, dst, f_send.at[1], recv, (below, to))))
+            act(remote(src, dst, f_send.at[2], recv, (side, to)))
+
+    part_rows = width // 2
+
+    def outgoing(core, t):
+        rows = pl.ds(pl.multiple_of((2 * q + core) * width + t * part_rows, part_rows), part_rows)
+        return core, t, own.at[rows, cols(far, c)], held.at[span(2 * o + t, part_rows), cols(far, c)]
 
     lend.wait_recv()
     own[:, cols(far, c)] = transform(full[...], raw[...])
-    hand_out(outgoing, start)
+    hand_out([outgoing(core, t) for t in range(2) for core in range(2)], start)
     far_part(c).start()
     own[:, cols(q, c)] = transform(full[...], ints[o])
     near_part(c).start()
@@ -617,44 +632,40 @@
     mine = pltpu.make_async_copy(own.at[span(s, width)], held.at[span(o, width)], o_sem)
     mine.start()
 
+    def far_piece(block, t):
+        return held.at[span(2 * block + t, part_rows), span(far, 2 * tile)]
+
     def arrive(block):
         ref = held.at[span(block, width), span(far, 2 * tile)]
-        remote(ref, ref, x_fwd, f_recv.at[block], (side, s)).wait_recv()
-
-    def pass_on(chain, act):
-        block = 2 * chain + low
-        ref = held.at[span(block, width), span(far, 2 * tile)]
-        recv = f_recv.at[block]
+        remote(ref, ref, x_fwd, f_recv.at[block, 0], (side, s)).wait_recv()
+
+    def arrive_pieces(block):
+        for t in range(2):
+            ref = far_piece(block, t)
+            remote(ref, ref, x_fwd, f_recv.at[block, t], (side, s)).wait_recv()
+
+    def pass_on(chain, ref, recv, act):
         pl.when(jnp.logical_and(chain < z, z < nz - 1))(lambda: act(remote(ref, ref, z_fwd.at[0], recv, (above, s))))
         pl.when(jnp.logical_and(chain > z, z > 0))(lambda: act(remote(ref, ref, z_fwd.at[1], recv, (below, s))))
         pl.when(chain == nearest(1))(lambda: act(remote(ref, ref, x_fwd, recv, (side, s))))
 
-    def beside_each(act):
-        pl.when(z > 0)(lambda: act(z - 1))
-        pl.when(z < nz - 1)(lambda: act(z + 1))
-
-    def take(chain):
-        arrive(2 * chain + low)
-        pass_on(chain, start)
-
-    beside_each(take)
+    def take(chain, t):
+        block = 2 * chain + low
+        ref = far_piece(block, t)
+        remote(ref, ref, x_fwd, f_recv.at[block, t], (side, s)).wait_recv()
+        pass_on(chain, ref, f_recv.at[block, t], start)
+
+    for t in range(2):
+        each_at(1, lambda chain: take(chain, t))
     given().wait_recv()
     mine.wait()
 
-    def absorb(chain):
-        rows = span(chain, 2 * width)
+    def absorb(slot, chain):
         coulomb = lax.dot_general(
-            held[rows, :], own[...], (((1,), (1,)), ((), ())), preferred_element_type=F32
+            held[span(chain, 2 * width), :], own[...], (((1,), (1,)), ((), ())), preferred_element_type=F32
         )
         left = jnp.concatenate([energies[o] + energies[2 * chain + t] - col_e for t in range(2)], axis=0)
-        amps[rows, :] = (coulomb / (left - row_e)).astype(jnp.bfloat16)
-
-    @pl.loop(0, nz)
-    def _(i):
-        chain = nearest(jnp.where(i == 0, 0, jnp.where(i == nz - 1, 1, i + 1)))
-        pl.when(jnp.abs(chain - z) > 1)(lambda: arrive(2 * chain + low))
-        arrive(2 * chain + 1 - low)
-        absorb(chain)
+        amps[slot * 2 * width : (slot + 1) * 2 * width, :] = (coulomb / (left - row_e)).astype(jnp.bfloat16)
 
     contract = (((0,), (0,)), ((), ()))
     strips, strip = t_give.shape[0], t_give.shape[-1]
@@ -664,10 +675,41 @@
     def wide(k):
         return pl.ds(k * strip, strip)
 
-    def part_three(group, core, where):
+    early, late = range(nz // 2), range(nz // 2, nz)
+
+    def amps_of(slots, where=slice(None)):
+        return amps[slots[0] * 2 * width : (slots[-1] + 1) * 2 * width, where]
+
+    def part_three(group, core, where, slots):
+        rows = [held[span(order[i], 2 * width), cols(group, core)] for i in slots]
         return lax.dot_general(
-            held[:, cols(group, core)], amps[:, where], contract, preferred_element_type=F32
-        )
+            jnp.concatenate(rows, axis=0), amps_of(slots, where), contract, preferred_element_type=F32
+        )
+
+    def part_vir(half, slots):
+        new = lax.dot_general(
+            amps_of(slots, span(half, middle)), amps_of(slots), contract, preferred_element_type=F32
+        )
+        return new.reshape((nz // 2,) + vir.shape[1:])
+
+    def admit(i):
+        chain = order[i]
+        pl.when(distant(chain))(lambda: arrive(2 * chain + low))
+        pl.when(jnp.abs(chain - z) == 2)(lambda: arrive_pieces(2 * chain + low))
+        passed = jnp.logical_or(chain == z, chain == nearest(1))
+        pl.when(passed)(lambda: arrive_pieces(2 * chain + 1 - low))
+        pl.when(jnp.logical_not(passed))(lambda: arrive(2 * chain + 1 - low))
+        absorb(i, chain)
+
+    for i in early:
+        admit(i)
+    for half in range(2):
+        vir[pl.ds(half * (nz // 2), nz // 2)] = part_vir(half, early)
+    for k in range(strips):
+        t_give[k] = part_three(far, 1 - c, wide(k), early)
+        t_mine[k] = part_three(far, c, wide(k), early)
+    for i in late:
+        admit(i)
 
     def far_swap(k):
         return remote(t_give.at[k], t_got.at[k], t_send, t_recv.at[k], partner)
@@ -728,10 +770,8 @@
     near_swap = remote(n_give, n_got, n_sems.at[0], n_sems.at[1], partner)
     first = jnp.where(z < nz // 2, 1, 0)
     for half in (first, 1 - first):
-        new = lax.dot_general(
-            amps[:, span(half, middle)], amps[...], contract, preferred_element_type=F32
-        )
-        vir[pl.ds(half * (nz // 2), nz // 2)] = new.reshape((nz // 2,) + vir.shape[1:])
+        where = pl.ds(half * (nz // 2), nz // 2)
+        vir[where] = vir[where] + part_vir(half, late)
         for t in range(nz // 2):
             v_swap(half * (nz // 2) + t).start()
 
@@ -747,12 +787,12 @@
 
     for k in range(max(strips, nz)):
         if k < strips:
-            t_give[k] = part_three(far, 1 - c, wide(k))
+            t_give[k] += part_three(far, 1 - c, wide(k), late)
             far_swap(k).start()
         if k < nz:
             add_pair(farthest[k])
     for k in range(strips):
-        new = part_three(far, c, wide(k))
+        new = t_mine[k] + part_three(far, c, wide(k), late)
         far_swap(k).wait_recv()
         encode(new + t_got[k], t_code.at[k], t_scale.at[k])
         both_start(far_send(k))
@@ -766,11 +806,11 @@
             both_start(along(chain, z))
 
     def near_give():
-        n_give[...] = part_three(q, 1 - c, slice(None))
+        n_give[...] = part_three(q, 1 - c, slice(None), range(nz))
         near_swap.start()
 
     def near_keep():
-        near_sum[...] = part_three(q, c, slice(None))
+        near_sum[...] = part_three(q, c, slice(None), range(nz))
 
     fillers = [near_give, near_keep]
     for k in range(nz):
@@ -809,7 +849,7 @@
 
     def lent(blocks, sem):
         ref = cross.at[:blocks]
-        return remote(ref, ref, y_send.at[sem], f_recv.at[0], opposite)
+        return remote(ref, ref, y_send.at[sem], f_recv.at[0, 0], opposite)
 
     if nz > 2:
         lent(nz - 2, 0).wait_send()
@@ -817,10 +857,11 @@
         pl.when(distant(nearest(k)))(lambda: lent(1, k - 1).wait_send())
 
     both_rows = own.at[: 2 * width, :tile]
-    hand_out([(0, both_rows, both_rows)], sent)
+    hand_out([(0, 0, both_rows, both_rows)], sent)
     far_part(c).wait_send()
     near_part(c).wait_send()
-    beside_each(lambda chain: pass_on(chain, sent))
+    block_ref = held.at[:width, : 2 * tile]
+    each_at(1, lambda chain: pass_on(chain, block_ref, f_recv.at[0, 0], sent))
     near_swap.wait_send()
     remote(t_give, t_give, t_send, t_recv.at[0], partner).wait_send()
     both_sent(coded_copies(t_code, t_scale, t_code, t_scale, (ts_send, ts_recv.at[0]), opposite))
@@ -855,7 +896,7 @@
         packed(n, tile, basis), packed(tile, basis), packed(virtuals, basis), packed(virtuals, 4 * tile),
         packed(n * width, 4 * tile), packed(n, width, tile), packed(n, 2 * width, tile), packed(n * width, virtuals),
         room(nz, 2, 2, 2, rows, virtuals),
-        room(strips, tile, strip), room(strips, tile, strip), room(tile, virtuals), room(tile, virtuals),
+        room(strips, tile, strip), room(strips, tile, strip), room(strips, tile, strip), room(tile, virtuals), room(tile, virtuals),
         room(tile, virtuals), room(nz, 2, 2, rows, virtuals), room(2 * rows, virtuals), room(2, rows, virtuals),
     ]
     groups = tile // 32
@@ -868,7 +909,7 @@
     scratch += [pltpu.SMEM((n,), F32), room(virtuals)]
     scratch += [
         dma((2,)), dma, dma, dma, dma((2,)), dma((n, pieces)), dma((2,)), dma((2,)), dma((nz,)), dma((2, nz)), dma((2,)),
-        dma((2,)), dma((2,)), dma((n,)), dma((3,)), dma((2,)), dma, dma((nz,)), dma((2,)),
+        dma((2,)), dma((2,)), dma((n, 2)), dma((3,)), dma((2,)), dma, dma((nz,)), dma((2,)),
         dma, dma((strips,)), dma((2,)), dma((strips, 2)), dma((2,)), dma, dma((nz,)),
         dma((2,)), dma((nz, 2)), dma((2,)), dma((nz, 2)), dma((2,)), dma((2,)),
     ]

time: 56.5 us -> 54.8 us (0.970)
  Pallas kernels: 54.2 us -> 52.5 us
    pallas_call x1, Pallas kernels: 54.2 us -> 52.5 us  [paired(): pl.pallas_call(functools.partial(paired_kernel, n), out_shape=(pltpu.VMEM...]
where the time goes in v5:
time: 54.8 us; the launch traced here: 54.6 us
  Pallas kernels  52.5 us (96%)
  local copies, waits for them, and re-layouts  1.51 us (3%)
  between operations  0.64 us (1%)
    pallas_call x1, Pallas kernels, paired(): pl.pallas_call(functools.partial(paired_kernel, n), out_shape=(pltpu.VMEM...  52.5 us
    unnamed x2, local copies, waits for them, and re-layouts  1.51 us

profile of v5, /device:TPU:0, one launch (start us, length us, event | category | flops | bytes accessed | tf_op | source)
XLA Modules:
  0.0 54.6 jit_solution(11409201771943244874)
XLA Ops:
  0.6 52.5 %densities.1 = (f32[256,1,768]{2,1,0:T(1,128)S(1)}, f32[24,768]{1,0:T(8,128)S(1)}) custom-call(f32[8]{0:T(128)} %occ_e.1, bf16[8,256,1024]{2,1,0:T(8,128)(2,1)} %half.1, bf16[96,1024]{1,0:T(8,128)(2,1)} %bitcast.1, f32[768]{0:T(1024)} %vir_e.1), custom_call_target="tpu_custom_call" | custom-call | tf_op jit(solution)/shard_map/densities/pallas_call | solution.py:916
  53.1 0.9 %copy.8 = f32[256,1,768]{2,1,0:T(1,128)} copy(f32[256,1,768]{2,1,0:T(1,128)S(1)} %get-tuple-element.2) | data formatting | bytes 1572864
  54.0 0.6 %copy.9 = f32[24,768]{1,0:T(8,128)} copy(f32[24,768]{1,0:T(8,128)S(1)} %get-tuple-element.3) | data formatting | bytes 147456

commit v6 on v5

--- a/solution.py
+++ b/solution.py
@@ -469,7 +469,6 @@
     pl.semaphore_wait(barrier, len(peers))
 
     lend = remote(half.at[o], raw, raw_sems.at[0], raw_sems.at[1], opposite)
-    lend.start()
 
     def coef_slot(block, core, h):
         return full.at[span(block, part), pl.ds(pl.multiple_of((pieces * core + h) * piece, piece), piece)]
@@ -507,6 +506,7 @@
         coef_relay(z, coef_own(h), coef_slot(o, c, h), c_recv.at[o, h], start)
     for h in range(pieces):
         coef_far(coef_own(h), coef_slot(o, c, h), c_recv.at[o, h], start)
+    lend.start()
     for copy in small:
         copy.wait()
     row_e = levels[...].reshape(1, virtuals)
@@ -530,15 +530,15 @@
         coef_relay(chain, slot, slot, c_recv.at[block, h], start)
         coef_across(block, h, c).start()
 
-    for d in range(1, nz + 1):
+    for h in range(pieces):
+        each_at(1, lambda chain: coef_along(chain, h))
+    for h in range(pieces):
+        coef_beside(z, h)
+        for d in list(range(3, nz)) + [2]:
+            each_at(d, lambda chain: coef_along(chain, h))
+    for d in [1] + list(range(3, nz)) + [2]:
         for h in range(pieces):
-            if d < nz:
-                each_at(d, lambda chain: coef_along(chain, h))
-        for h in range(pieces):
-            if d == 1:
-                coef_beside(z, h)
-            else:
-                each_at(d - 1, lambda chain: coef_beside(chain, h))
+            each_at(d, lambda chain: coef_beside(chain, h))
 
     def coef_halves(blocks):
         ref = full.at[: blocks * part, : basis // 2]

time: 54.8 us -> 53.7 us (0.980)
  Pallas kernels: 52.5 us -> 51.4 us
    pallas_call x1, Pallas kernels: 52.5 us -> 51.4 us  [paired(): pl.pallas_call(functools.partial(paired_kernel, n), out_shape=(pltpu.VMEM...]
where the time goes in v6:
time: 53.7 us; the launch traced here: 53.5 us
  Pallas kernels  51.4 us (96%)
  local copies, waits for them, and re-layouts  1.51 us (3%)
  between operations  0.64 us (1%)
    pallas_call x1, Pallas kernels, paired(): pl.pallas_call(functools.partial(paired_kernel, n), out_shape=(pltpu.VMEM...  51.4 us
    unnamed x2, local copies, waits for them, and re-layouts  1.51 us

profile of v6, /device:TPU:0, one launch (start us, length us, event | category | flops | bytes accessed | tf_op | source)
XLA Modules:
  0.0 53.5 jit_solution(13257680602370656700)
XLA Ops:
  0.6 51.4 %densities.1 = (f32[256,1,768]{2,1,0:T(1,128)S(1)}, f32[24,768]{1,0:T(8,128)S(1)}) custom-call(f32[8]{0:T(128)} %occ_e.1, bf16[8,256,1024]{2,1,0:T(8,128)(2,1)} %half.1, bf16[96,1024]{1,0:T(8,128)(2,1)} %bitcast.1, f32[768]{0:T(1024)} %vir_e.1), custom_call_target="tpu_custom_call" | custom-call | tf_op jit(solution)/shard_map/densities/pallas_call | solution.py:916
  52.0 0.9 %copy.8 = f32[256,1,768]{2,1,0:T(1,128)} copy(f32[256,1,768]{2,1,0:T(1,128)S(1)} %get-tuple-element.2) | data formatting | bytes 1572864
  52.9 0.6 %copy.9 = f32[24,768]{1,0:T(8,128)} copy(f32[24,768]{1,0:T(8,128)S(1)} %get-tuple-element.3) | data formatting | bytes 147456

commit v7 on v6

--- a/solution.py
+++ b/solution.py
@@ -412,7 +412,7 @@
 
 def paired_kernel(
     n, occ_e, half, coef, vir_e, three_out, vir_out,
-    ints, raw, full, own, held, gift, cross, amps, vir,
+    ints, raw, full, own, held, gift, cross, amps, base, vir,
     t_give, t_mine, t_got, n_give, n_got, near_sum, v_pair, v_line, v_col,
     t_code, t_scale, t_code_in, t_scale_in, x_code, x_scale, x_code_in, x_scale_in,
     z_code, z_scale, z_code_in, z_scale_in, y_code, y_scale, y_code_in, y_scale_in, energies, levels,
@@ -496,10 +496,10 @@
     def coef_far(src, dst, recv, act):
         for d in range(3, nz):
             pl.when(z + d < nz)(
-                lambda: act(remote(src, dst, c_jump.at[0, d], recv, (o + 2 * d, s)))
+                lambda: act(remote(src, dst, c_jump.at[0, d - 3], recv, (o + 2 * d, s)))
             )
             pl.when(z >= d)(
-                lambda: act(remote(src, dst, c_jump.at[1, d], recv, (o - 2 * d, s)))
+                lambda: act(remote(src, dst, c_jump.at[1, d - 3], recv, (o - 2 * d, s)))
             )
 
     for h in range(pieces):
@@ -660,10 +660,19 @@
     given().wait_recv()
     mine.wait()
 
+    def overlap(chain, group):
+        where = span(group, 2 * tile)
+        return lax.dot_general(
+            held[span(chain, 2 * width), where], own[:, where], (((1,), (1,)), ((), ())), preferred_element_type=F32
+        )
+
     def absorb(slot, chain):
-        coulomb = lax.dot_general(
-            held[span(chain, 2 * width), :], own[...], (((1,), (1,)), ((), ())), preferred_element_type=F32
-        )
+        if slot:
+            coulomb = base[slot - 1] + overlap(chain, far)
+        else:
+            coulomb = lax.dot_general(
+                held[span(chain, 2 * width), :], own[...], (((1,), (1,)), ((), ())), preferred_element_type=F32
+            )
         left = jnp.concatenate([energies[o] + energies[2 * chain + t] - col_e for t in range(2)], axis=0)
         amps[slot * 2 * width : (slot + 1) * 2 * width, :] = (coulomb / (left - row_e)).astype(jnp.bfloat16)
 
@@ -701,7 +710,10 @@
         pl.when(jnp.logical_not(passed))(lambda: arrive(2 * chain + 1 - low))
         absorb(i, chain)
 
-    for i in early:
+    admit(0)
+    for i in range(1, nz):
+        base[i - 1] = overlap(order[i], q)
+    for i in early[1:]:
         admit(i)
     for half in range(2):
         vir[pl.ds(half * (nz // 2), nz // 2)] = part_vir(half, early)
@@ -895,20 +907,21 @@
     scratch = [
         packed(n, tile, basis), packed(tile, basis), packed(virtuals, basis), packed(virtuals, 4 * tile),
         packed(n * width, 4 * tile), packed(n, width, tile), packed(n, 2 * width, tile), packed(n * width, virtuals),
+        room(nz - 1, 2 * width, virtuals),
         room(nz, 2, 2, 2, rows, virtuals),
         room(strips, tile, strip), room(strips, tile, strip), room(strips, tile, strip), room(tile, virtuals), room(tile, virtuals),
         room(tile, virtuals), room(nz, 2, 2, rows, virtuals), room(2 * rows, virtuals), room(2, rows, virtuals),
     ]
-    groups = tile // 32
+    groups = tile // 64
     for _ in range(2):
         scratch += [packed(strips, tile, strip), room(strips, groups, 1, strip)]
     for _ in range(4):
-        scratch += [packed(nz, 2 * rows, virtuals), room(nz, 2, 1, virtuals)]
+        scratch += [packed(nz, 2 * rows, virtuals), room(nz, 1, 1, virtuals)]
     for _ in range(2):
         scratch += [packed(rows, virtuals), room(1, 1, virtuals)]
     scratch += [pltpu.SMEM((n,), F32), room(virtuals)]
     scratch += [
-        dma((2,)), dma, dma, dma, dma((2,)), dma((n, pieces)), dma((2,)), dma((2,)), dma((nz,)), dma((2, nz)), dma((2,)),
+        dma((2,)), dma, dma, dma, dma((2,)), dma((n, pieces)), dma((2,)), dma((2,)), dma((nz,)), dma((2, max(nz - 3, 1))), dma((2,)),
         dma((2,)), dma((2,)), dma((n, 2)), dma((3,)), dma((2,)), dma, dma((nz,)), dma((2,)),
         dma, dma((strips,)), dma((2,)), dma((strips, 2)), dma((2,)), dma, dma((nz,)),
         dma((2,)), dma((nz, 2)), dma((2,)), dma((nz, 2)), dma((2,)), dma((2,)),
@@ -934,7 +947,7 @@
     _, tile, basis = half_integrals.shape
     part = vir_coef.shape[1]
     virtuals = part * n
-    if nq == 2 and n % 2 == 0 and nz > 1 and nz % 2 == 0 and virtuals % (32 * n) == 0 and virtuals % 256 == 0 and tile % 32 == 0:
+    if nq == 2 and n % 2 == 0 and nz > 1 and nz % 2 == 0 and virtuals % (32 * n) == 0 and virtuals % 256 == 0 and tile % 64 == 0:
         three, vir_rows = paired(n, half_integrals, vir_coef.T, occ_energy, vir_energy)
         return three, vir_rows
     width, rows = virtuals // aux, virtuals // (n * aux)

time: 53.7 us -> 52.8 us (0.983)
  Pallas kernels: 51.4 us -> 50.4 us
    pallas_call x1, Pallas kernels: 51.4 us -> 50.4 us  [paired(): pl.pallas_call(functools.partial(paired_kernel, n), out_shape=(pltpu.VMEM...]
where the time goes in v7:
time: 52.8 us; the launch traced here: 52.6 us
  Pallas kernels  50.4 us (95%)
  local copies, waits for them, and re-layouts  1.51 us (3%)
  between operations  0.64 us (1%)
    pallas_call x1, Pallas kernels, paired(): pl.pallas_call(functools.partial(paired_kernel, n), out_shape=(pltpu.VMEM...  50.4 us
    unnamed x2, local copies, waits for them, and re-layouts  1.51 us

profile of v7, /device:TPU:0, one launch (start us, length us, event | category | flops | bytes accessed | tf_op | source)
XLA Modules:
  0.0 52.6 jit_solution(5660002621170711322)
XLA Ops:
  0.6 50.4 %densities.1 = (f32[256,1,768]{2,1,0:T(1,128)S(1)}, f32[24,768]{1,0:T(8,128)S(1)}) custom-call(f32[8]{0:T(128)} %occ_e.1, bf16[8,256,1024]{2,1,0:T(8,128)(2,1)} %half.1, bf16[96,1024]{1,0:T(8,128)(2,1)} %bitcast.1, f32[768]{0:T(1024)} %vir_e.1), custom_call_target="tpu_custom_call" | custom-call | tf_op jit(solution)/shard_map/densities/pallas_call | solution.py:929
  51.1 0.9 %copy.8 = f32[256,1,768]{2,1,0:T(1,128)} copy(f32[256,1,768]{2,1,0:T(1,128)S(1)} %get-tuple-element.2) | data formatting | bytes 1572864
  52.0 0.6 %copy.9 = f32[24,768]{1,0:T(8,128)} copy(f32[24,768]{1,0:T(8,128)S(1)} %get-tuple-element.3) | data formatting | bytes 147456

commit v8 on v7

--- a/solution.py
+++ b/solution.py
@@ -418,7 +418,7 @@
     z_code, z_scale, z_code_in, z_scale_in, y_code, y_scale, y_code_in, y_scale_in, energies, levels,
     e_sems, i_sem, keep_sem, o_sem, raw_sems, c_recv, c_up, c_down, c_side, c_jump, cp_sems,
     pn_sems, pf_sems, f_recv, f_send, z_fwd, x_fwd, y_send, g_sems,
-    t_send, t_recv, ts_send, ts_recv, n_sems, vp_send, vp_recv, x_send, x_recv, z_send, z_recv, yv_send, yv_recv,
+    t_send, ts_send, n_sems, vp_send, x_send, z_send, z_recv, yv_send, yv_recv,
 ):
     o = lax.axis_index("occ")
     s = lax.axis_index("aux")
@@ -724,7 +724,7 @@
         admit(i)
 
     def far_swap(k):
-        return remote(t_give.at[k], t_got.at[k], t_send, t_recv.at[k], partner)
+        return remote(t_give.at[k], t_got.at[k], t_send, c_recv.at[nz + k, 2], partner)
 
     def coded_copies(code, scale, code_to, scale_to, sems, target):
         return (
@@ -733,11 +733,11 @@
         )
 
     def far_send(k):
-        sems = (ts_send, ts_recv.at[k])
+        sems = (ts_send, c_recv.at[nz + k])
         return coded_copies(t_code.at[k], t_scale.at[k], t_code_in.at[k], t_scale_in.at[k], sems, opposite)
 
     def x_swap(chain):
-        sems = (x_send, x_recv.at[chain])
+        sems = (x_send, c_recv.at[chain])
         return coded_copies(
             x_code.at[chain], x_scale.at[chain], x_code_in.at[chain], x_scale_in.at[chain], sems, (side, s)
         )
@@ -774,7 +774,7 @@
         return (words * (scale[...] * (1.0 / SPAN))).reshape(code.shape)
 
     def v_swap(chain):
-        return remote(vir.at[chain, :, :, 1 - c], v_pair.at[chain], vp_send, vp_recv.at[chain], partner)
+        return remote(vir.at[chain, :, :, 1 - c], v_pair.at[chain], vp_send, c_recv.at[chain, 2], partner)
 
     def between():
         return coded_copies(y_code, y_scale, y_code_in, y_scale_in, (yv_send, yv_recv), opposite)
@@ -875,11 +875,11 @@
     block_ref = held.at[:width, : 2 * tile]
     each_at(1, lambda chain: pass_on(chain, block_ref, f_recv.at[0, 0], sent))
     near_swap.wait_send()
-    remote(t_give, t_give, t_send, t_recv.at[0], partner).wait_send()
-    both_sent(coded_copies(t_code, t_scale, t_code, t_scale, (ts_send, ts_recv.at[0]), opposite))
+    remote(t_give, t_give, t_send, c_recv.at[nz, 2], partner).wait_send()
+    both_sent(coded_copies(t_code, t_scale, t_code, t_scale, (ts_send, c_recv.at[nz]), opposite))
     whole = vir.at[:, :, :, 0]
-    remote(whole, whole, vp_send, vp_recv.at[0], partner).wait_send()
-    both_sent(coded_copies(x_code, x_scale, x_code, x_scale, (x_send, x_recv.at[0]), (side, s)))
+    remote(whole, whole, vp_send, c_recv.at[0, 2], partner).wait_send()
+    both_sent(coded_copies(x_code, x_scale, x_code, x_scale, (x_send, c_recv.at[0]), (side, s)))
     codes, scales = z_code.at[: nz - 1], z_scale.at[: nz - 1]
     both_sent(coded_copies(codes, scales, codes, scales, (z_send, z_recv.at[0]), (side, s)))
     both_sent(between())
@@ -923,8 +923,7 @@
     scratch += [
         dma((2,)), dma, dma, dma, dma((2,)), dma((n, pieces)), dma((2,)), dma((2,)), dma((nz,)), dma((2, max(nz - 3, 1))), dma((2,)),
         dma((2,)), dma((2,)), dma((n, 2)), dma((3,)), dma((2,)), dma, dma((nz,)), dma((2,)),
-        dma, dma((strips,)), dma((2,)), dma((strips, 2)), dma((2,)), dma, dma((nz,)),
-        dma((2,)), dma((nz, 2)), dma((2,)), dma((nz, 2)), dma((2,)), dma((2,)),
+        dma, dma((2,)), dma((2,)), dma, dma((2,)), dma((2,)), dma((nz, 2)), dma((2,)), dma((2,)),
     ]
     return pl.pallas_call(
         functools.partial(paired_kernel, n),
@@ -947,7 +946,7 @@
     _, tile, basis = half_integrals.shape
     part = vir_coef.shape[1]
     virtuals = part * n
-    if nq == 2 and n % 2 == 0 and nz > 1 and nz % 2 == 0 and virtuals % (32 * n) == 0 and virtuals % 256 == 0 and tile % 64 == 0:
+    if nq == 2 and n % 2 == 0 and nz > 1 and nz % 2 == 0 and virtuals % (32 * n) == 0 and virtuals % 256 == 0 and tile % 64 == 0 and basis % (256 * PIECES) == 0 and nz >= virtuals // 256:
         three, vir_rows = paired(n, half_integrals, vir_coef.T, occ_energy, vir_energy)
         return three, vir_rows
     width, rows = virtuals // aux, virtuals // (n * aux)

time: 52.8 us -> 52.6 us (level)
  no operation moved by 1% of the time
where the time goes in v8:
time: 52.6 us; the launch traced here: 52.4 us
  Pallas kernels  50.3 us (96%)
  local copies, waits for them, and re-layouts  1.51 us (3%)
  between operations  0.64 us (1%)
    pallas_call x1, Pallas kernels, paired(): pl.pallas_call(functools.partial(paired_kernel, n), out_shape=(pltpu.VMEM...  50.3 us
    unnamed x2, local copies, waits for them, and re-layouts  1.51 us

profile of v8, /device:TPU:0, one launch (start us, length us, event | category | flops | bytes accessed | tf_op | source)
XLA Modules:
  0.0 52.4 jit_solution(6315322136115665894)
XLA Ops:
  0.6 50.3 %densities.1 = (f32[256,1,768]{2,1,0:T(1,128)S(1)}, f32[24,768]{1,0:T(8,128)S(1)}) custom-call(f32[8]{0:T(128)} %occ_e.1, bf16[8,256,1024]{2,1,0:T(8,128)(2,1)} %half.1, bf16[96,1024]{1,0:T(8,128)(2,1)} %bitcast.1, f32[768]{0:T(1024)} %vir_e.1), custom_call_target="tpu_custom_call" | custom-call | tf_op jit(solution)/shard_map/densities/pallas_call | solution.py:928
  50.9 0.9 %copy.8 = f32[256,1,768]{2,1,0:T(1,128)} copy(f32[256,1,768]{2,1,0:T(1,128)S(1)} %get-tuple-element.2) | data formatting | bytes 1572864
  51.8 0.6 %copy.9 = f32[24,768]{1,0:T(8,128)} copy(f32[24,768]{1,0:T(8,128)S(1)} %get-tuple-element.3) | data formatting | bytes 147456
